TPU v7x, 768 devices: a whole 4x8x12 slice. The times are simulated.
768 devices in a mesh: mode: 16 (over x_hi, y), tile: 48 (over z, x_lo, core).
Axes of the slice: x: 4 (x_hi: 2, x_lo: 2; x = x_hi * 2 + x_lo), y: 8, z: 12, core: 2. Of those that a mesh axis runs over, the one named last changes fastest.
Arguments:
- velocity: float32 [128, 3, 196608], P('mode', None, 'tile'), may hold values from -6 to 6
- vorticity: float32 [128, 3, 196608], P('mode', None, 'tile'), may hold values from -6 to 6
- viscosity: float32 [2], replicated, may hold values from 0.1 to 0.4
Outputs:
- rate: float32 [128, 3, 196608], P('mode', None, 'tile')
All inputs are finite; a program needn't handle non-finite values.
Results may differ from a plain program's by a relative error of at most 0.0001.
Values sent between devices are 32-bit elements; how exact they have to be, the bound alone decides.
A program may use at most 32 MiB of HBM per device.

v0:
```python
import math

import jax
import jax.numpy as jnp
import numpy as np
from jax import lax
from jax.sharding import PartitionSpec as P

MODES = 8
NY = 1024


def padded(block, sides, width):
    for axis, dim in sides:
        count = lax.axis_size(axis)
        forward = [(i, i + 1) for i in range(count - 1)]
        forward.append((count - 1, 0))
        backward = [(target, source) for source, target in forward]
        low = lax.ppermute(
            lax.slice_in_dim(block, block.shape[dim] - width, None, axis=dim), axis, forward
        )
        high = lax.ppermute(lax.slice_in_dim(block, 0, width, axis=dim), axis, backward)
        block = jnp.concatenate([low, block, high], axis=dim)
    return block


def legendre_list(count, where):
    values_list = [1.0, where]
    for degree in range(1, count):
        values_list.append(
            ((2 * degree + 1) * where * values_list[degree] - degree * values_list[degree - 1])
            / (degree + 1)
        )
    return values_list


def gauss_nodes(order):
    nodes_list = []
    weights_list = []
    for number in range(order):
        guess = math.cos(math.pi * (number + 0.75) / (order + 0.5))
        for sweep in range(60):
            values_list = legendre_list(order, guess)
            slope = (
                order
                * (guess * values_list[order] - values_list[order - 1])
                / (guess * guess - 1.0)
            )
            guess = guess - values_list[order] / slope
        values_list = legendre_list(order, guess)
        slope = (
            order * (guess * values_list[order] - values_list[order - 1]) / (guess * guess - 1.0)
        )
        nodes_list.append(guess)
        weights_list.append(2.0 / ((1.0 - guess * guess) * slope * slope))
    return (nodes_list, weights_list)


def triple_table(mode_count):
    nodes_list, weights_list = gauss_nodes(2 * mode_count)
    scaled = [
        [
            math.sqrt(2.0 * degree + 1.0) * legendre_list(mode_count, node_value)[degree]
            for degree in range(mode_count)
        ]
        for node_value in nodes_list
    ]
    table = [
        [
            [
                0.5
                * sum(
                    (
                        weights_list[number]
                        * scaled[number][first]
                        * scaled[number][second]
                        * scaled[number][third]
                        for number in range(len(nodes_list))
                    )
                )
                for third in range(mode_count)
            ]
            for second in range(mode_count)
        ]
        for first in range(mode_count)
    ]
    return np.array(table)


def cross_along(left_vec, right_vec, direction):

    def component(vector, number):
        return lax.index_in_dim(vector, number, direction, keepdims=False)

    components = [
        component(left_vec, 1) * component(right_vec, 2)
        - component(left_vec, 2) * component(right_vec, 1),
        component(left_vec, 2) * component(right_vec, 0)
        - component(left_vec, 0) * component(right_vec, 2),
        component(left_vec, 0) * component(right_vec, 1)
        - component(left_vec, 1) * component(right_vec, 0),
    ]
    return jnp.stack(components, axis=direction)


def centred(source_field, direction):
    return 0.5 * (jnp.roll(source_field, -1, direction) - jnp.roll(source_field, 1, direction))


def second_diff(source_field, direction):
    return (
        jnp.roll(source_field, -1, direction)
        + jnp.roll(source_field, 1, direction)
        - 2.0 * source_field
    )


def rim_dx(rimmed):
    return 0.5 * (rimmed[:, 2:] - rimmed[:, :-2])


def core_dy(rimmed):
    return centred(rimmed[:, 1:-1], 2)


def plane_laplace(rimmed):
    inner = rimmed[:, 1:-1]
    return (
        rimmed[:, 2:]
        + rimmed[:, :-2]
        + jnp.roll(inner, -1, 2)
        + jnp.roll(inner, 1, 2)
        - 4.0 * inner
    )


def shards(velocity, vorticity, viscosity):
    row_count = velocity.shape[0]
    cell_count = velocity.shape[2]
    slab_rows = cell_count // NY
    group_count = lax.axis_size("mode")
    piece_cells = cell_count // group_count
    planes = row_count * group_count // MODES
    coupling = jnp.asarray(triple_table(MODES), dtype=jnp.float32)
    mixing = viscosity[0] * coupling[0] + viscosity[1] * coupling[1]
    flat_coupling = jnp.transpose(coupling, (0, 2, 1)).reshape(MODES * MODES, MODES)
    mixing_rows = jnp.transpose(mixing)

    def split_cells(source_field):
        return source_field.reshape(row_count, source_field.shape[1], group_count, piece_cells)

    speed_modes = lax.all_to_all(
        split_cells(velocity), "mode", split_axis=2, concat_axis=0, tiled=True
    )
    width_cells = speed_modes.shape[3]
    speed_four = speed_modes.reshape(MODES, planes, 3, width_cells)
    spin_flat = lax.all_to_all(
        split_cells(vorticity), "mode", split_axis=2, concat_axis=0, tiled=True
    ).reshape(MODES, planes * 3 * width_cells)
    mixed_spin = jnp.dot(flat_coupling, spin_flat, precision=lax.Precision.HIGHEST).reshape(
        MODES, MODES, planes, 3, width_cells
    )
    flux_terms = jnp.sum(cross_along(speed_four[:, None], mixed_spin, 3), axis=0)
    damped = jnp.dot(mixing_rows, spin_flat, precision=lax.Precision.HIGHEST).reshape(
        MODES, planes, 3, width_cells
    )
    flux_terms, damped, width_cells = (flux_terms, damped, width_cells)
    extra_first = -centred(flux_terms[:, :, 1], 1) + second_diff(damped[:, :, 0], 1)
    extra_second = centred(flux_terms[:, :, 0], 1) + second_diff(damped[:, :, 1], 1)
    extra_third = second_diff(damped[:, :, 2], 1)
    extras = jnp.stack([extra_first, extra_second, extra_third], axis=2)
    bundle = jnp.concatenate([flux_terms, damped, extras], axis=2).reshape(
        MODES * planes, 9, 1, width_cells
    )
    returned = lax.all_to_all(bundle, "mode", split_axis=0, concat_axis=2, tiled=True)
    returned = returned.reshape(row_count, 9, slab_rows, NY)
    rimmed = padded(returned[:, :6], (("tile", 2),), 1)
    flux_x = rimmed[:, 0]
    flux_y = rimmed[:, 1]
    flux_z = rimmed[:, 2]
    rate_x = core_dy(flux_z) + returned[:, 6] + plane_laplace(rimmed[:, 3])
    rate_y = -rim_dx(flux_z) + returned[:, 7] + plane_laplace(rimmed[:, 4])
    rate_z = rim_dx(flux_y) - core_dy(flux_x) + returned[:, 8] + plane_laplace(rimmed[:, 5])
    result = jnp.stack([rate_x, rate_y, rate_z], axis=1)
    return result.reshape(row_count, 3, cell_count)


def solution(mesh):
    in_specs = (P("mode", None, "tile"), P("mode", None, "tile"), P())
    out_specs = P("mode", None, "tile")
    return jax.shard_map(shards, mesh=mesh, in_specs=in_specs, out_specs=out_specs, check_vma=False)
```

profile of v0, /device:TPU:8, one launch (start us, length us, event | category | flops | bytes accessed | tf_op | source)
XLA Modules:
  0.0 110.7 jit_solution(4273510898642702314)
XLA Ops:
  0.0 0.0 copy-start
  0.0 1.8 %copy.158 = f32[3,1,16,8,256]{4,3,1,0,2:T(8,128)} copy(f32[3,1,16,8,256]{4,3,2,1,0:T(8,128)} %bitcast.210) | data formatting | bytes 786432 | tf_op jit(solution)/shard_map/reshape | solution.py:150
  1.8 0.0 copy-start.4
  1.8 12.9 %all-to-all-start = ((f32[8,3,16,256]{3,0,1,2:T(8,128)}), f32[8,3,16,256]{3,0,1,2:T(8,128)S(1)}, u32[]{:S(2)}, u32[]{:S(2)}) async-start(f32[8,3,16,256]{3,0,1,2:T(8,128)} %bitcast.198), calls=%async_computation | async-start | bytes 786432 | tf_op jit(solution)/shard_map/all_to_all | solution.py:152
  14.7 0.0 copy-done
  14.7 0.8 copy.157
  15.5 10.8 %all-to-all-done = f32[8,3,16,256]{3,0,1,2:T(8,128)S(1)} async-done(((f32[8,3,16,256]{3,0,1,2:T(8,128)}), f32[8,3,16,256]{3,0,1,2:T(8,128)S(1)}, u32[]{:S(2)}, u32[]{:S(2)}) %all-to-all-start) | async-done | bytes 393248 | tf_op jit(solution)/shard_map/all_to_all | solution.py:152
  26.3 4.6 %all-to-all-start.1 = ((f32[8,3,16,256]{3,0,1,2:T(8,128)}), f32[8,3,16,256]{3,0,1,2:T(8,128)S(1)}, u32[]{:S(2)}, u32[]{:S(2)}) async-start(f32[8,3,16,256]{3,0,1,2:T(8,128)} %bitcast.197), calls=%async_computation.1 | async-start | bytes 786432 | tf_op jit(solution)/shard_map/all_to_all | solution.py:157
  30.9 0.0 copy-done.4
  31.0 0.6 fusion.52
  31.6 0.0 copy-start.1
  31.6 10.7 %all-to-all-done.1 = f32[8,3,16,256]{3,0,1,2:T(8,128)S(1)} async-done(((f32[8,3,16,256]{3,0,1,2:T(8,128)}), f32[8,3,16,256]{3,0,1,2:T(8,128)S(1)}, u32[]{:S(2)}, u32[]{:S(2)}) %all-to-all-start.1) | async-done | bytes 393248 | tf_op jit(solution)/shard_map/all_to_all | solution.py:157
  42.4 0.2 copy.108
  42.6 0.3 reshape.325
  42.8 0.0 copy-done.1
  42.9 2.6 %fusion.53 = f32[8,8,16,3,256]{4,1,3,2,0:T(8,128)S(1)} fusion(f32[8,8,8,1,1]{2,1,4,3,0:T(8,128)S(1)} %copy-done.1, f32[16,3,256,8,1]{2,3,1,0,4:T(8,128)S(1)} %bitcast.201), kind=kOutput, calls=%fused_computation.119 | convolution fusion | flops 75497472 | bytes 3540992 | tf_op jit(solution)/shard_map/dot_general | solution.py:160
  45.4 0.5 multiply_subtract_fusion.2
  45.9 0.2 maximum_reduce_fusion
  46.2 0.0 copy-start.2
  46.2 0.0 copy-start.3
  46.3 0.6 copy-done.2
  46.8 0.0 copy-done.3
  46.9 1.8 %fusion.34 = f32[8,16,3,256]{3,0,2,1:T(8,128)S(1)} fusion(f32[16,3,256,8]{2,3,1,0:T(8,128)S(1)} %bitcast.202, f32[1,8,8]{2,1,0:T(8,128)S(1)} %copy-done.3, f32[1,8,8]{2,1,0:T(8,128)S(1)} %copy-done.2, f32[]{:T(128)} %bitcast.17, f32[]{:T(128)} %bitcast.16), kind=kOutput, calls=%fused_computation.100 | convolution fusion | flops 9437376 | bytes 786952 | tf_op jit(solution)/shard_map/dot_general | solution.py:164
  48.7 0.1 fusion.31
  48.9 0.1 copy.109
  49.0 0.1 copy.111
  49.2 0.1 fusion.27
  49.5 1.2 %copy.131 = f32[128,9,1,256]{3,2,1,0:T(1,128)S(1)} copy(f32[128,9,1,256]{3,0,1,2:T(8,128)S(1)} %constant_dynamic-update-slice_fusion) | data formatting | bytes 2359296 | tf_op jit(solution)/shard_map/concatenate | solution.py:172
  50.7 31.4 %all_to_all.45 = f32[128,9,1,256]{3,2,1,0:T(1,128)S(1)} all-to-all(f32[128,9,1,256]{3,2,1,0:T(1,128)S(1)} %copy.131), channel_id=1, replica_groups=mesh['mode'=16,'tile'=48] {'mode'}, dimensions={0} | all-to-all | bytes 2359296 | tf_op jit(solution)/shard_map/all_to_all | solution.py:175
  82.1 0.4 copy.156
  82.5 0.6 reshape.326
  83.0 0.3 fusion.41
  83.4 1.9 %collective-permute-start = (f32[8,6,1,1024]{3,2,0,1:T(1,128)S(1)}, f32[8,6,1,1024]{3,2,0,1:T(1,128)S(1)}, u32[]{:S(2)}, u32[]{:S(2)}) collective-permute-start(f32[8,6,1,1024]{3,2,0,1:T(1,128)S(1)} %copy.144), channel_id=1, source_target_pairs={{0,1},{1,2},{2,3},{3,4},{4,5},{5,6},{6,7},{7,8},{8,9},{9,10},{10,1... | collective-permute-start | bytes 589832 | tf_op jit(solution)/shard_map/ppermute | solution.py:19
  85.3 18.7 %collective-permute-start.1 = (f32[8,6,1,1024]{3,2,0,1:T(1,128)S(1)}, f32[8,6,1,1024]{3,2,0,1:T(1,128)S(1)}, u32[]{:S(2)}, u32[]{:S(2)}) collective-permute-start(f32[8,6,1,1024]{3,2,0,1:T(1,128)S(1)} %copy.146), channel_id=1, source_target_pairs={{1,0},{2,1},{3,2},{4,3},{5,4},{6,5},{7,6},{8,7},{9,8},{10,9},{11,1... | collective-permute-start | bytes 589832 | tf_op jit(solution)/shard_map/ppermute | solution.py:22
  104.0 1.4 %collective-permute-done = f32[8,6,1,1024]{3,2,0,1:T(1,128)S(1)} collective-permute-done((f32[8,6,1,1024]{3,2,0,1:T(1,128)S(1)}, f32[8,6,1,1024]{3,2,0,1:T(1,128)S(1)}, u32[]{:S(2)}, u32[]{:S(2)}) %collective-permute-start) | collective-permute-done | bytes 196640 | tf_op jit(solution)/shard_map/ppermute | solution.py:19
  105.4 1.8 %collective-permute-done.1 = f32[8,6,1,1024]{3,2,0,1:T(1,128)S(1)} collective-permute-done((f32[8,6,1,1024]{3,2,0,1:T(1,128)S(1)}, f32[8,6,1,1024]{3,2,0,1:T(1,128)S(1)}, u32[]{:S(2)}, u32[]{:S(2)}) %collective-permute-start.1) | collective-permute-done | bytes 196640 | tf_op jit(solution)/shard_map/ppermute | solution.py:22
  107.2 0.5 pad_maximum_fusion
  107.7 0.2 slice_bitcast_fusion.4
  107.8 0.1 fusion.43
  108.0 0.1 fusion.42
  108.1 0.1 fusion.45
  108.2 0.1 fusion.44
  108.3 0.1 fusion.47
  108.4 0.1 fusion.46
  108.5 0.1 fusion.49
  108.7 0.1 fusion.48
  108.7 0.1 fusion.51
  108.9 0.1 fusion.50
  109.0 0.2 fusion.15
  109.2 0.1 stack.22
  109.3 0.2 fusion.8
  109.5 0.1 stack.23
  109.6 0.3 fusion.1
  109.9 0.1 stack.24
  110.0 0.8 pad_maximum_fusion.1
  (21 shorter events, 0.5 us)
Async XLA Ops:
  0.0 14.7 %copy-start = (f32[8,3,4096]{2,0,1:T(8,128)S(1)}, f32[8,3,4096]{2,0,1:T(8,128)}, u32[]{:S(2)}) copy-start(f32[8,3,4096]{2,0,1:T(8,128)} %param.5) | copy-start | bytes 1179652
  1.8 29.1 %copy-start.4 = (f32[2]{0:T(128)S(1)}, f32[2]{0:T(128)}, u32[]{:S(2)}) copy-start(f32[2]{0:T(128)} %param.6) | copy-start | bytes 28
  1.8 24.5 %all-to-all-start = ((f32[8,3,16,256]{3,0,1,2:T(8,128)}), f32[8,3,16,256]{3,0,1,2:T(8,128)S(1)}, u32[]{:S(2)}, u32[]{:S(2)}) async-start(f32[8,3,16,256]{3,0,1,2:T(8,128)} %bitcast.198), calls=%async_computation | async-start | bytes 786432 | tf_op jit(solution)/shard_map/all_to_all | solution.py:152
  26.3 16.1 %all-to-all-start.1 = ((f32[8,3,16,256]{3,0,1,2:T(8,128)}), f32[8,3,16,256]{3,0,1,2:T(8,128)S(1)}, u32[]{:S(2)}, u32[]{:S(2)}) async-start(f32[8,3,16,256]{3,0,1,2:T(8,128)} %bitcast.197), calls=%async_computation.1 | async-start | bytes 786432 | tf_op jit(solution)/shard_map/all_to_all | solution.py:157
  31.6 11.3 %copy-start.1 = (f32[8,8,8,1,1]{2,1,4,3,0:T(8,128)S(1)}, f32[8,8,8,1,1]{2,1,4,3,0:T(8,128)}, u32[]{:S(2)}) copy-start(f32[8,8,8,1,1]{2,1,4,3,0:T(8,128)} %constant.17) | copy-start | bytes 6148
  46.2 0.7 copy-start.2
  46.2 0.7 copy-start.3
  83.4 22.0 %collective-permute-start = (f32[8,6,1,1024]{3,2,0,1:T(1,128)S(1)}, f32[8,6,1,1024]{3,2,0,1:T(1,128)S(1)}, u32[]{:S(2)}, u32[]{:S(2)}) collective-permute-start(f32[8,6,1,1024]{3,2,0,1:T(1,128)S(1)} %copy.144), channel_id=1, source_target_pairs={{0,1},{1,2},{2,3},{3,4},{4,5},{5,6},{6,7},{7,8},{8,9},{9,10},{10,1... | collective-permute-start | bytes 589832 | tf_op jit(solution)/shard_map/ppermute | solution.py:19
  85.3 21.8 %collective-permute-start.1 = (f32[8,6,1,1024]{3,2,0,1:T(1,128)S(1)}, f32[8,6,1,1024]{3,2,0,1:T(1,128)S(1)}, u32[]{:S(2)}, u32[]{:S(2)}) collective-permute-start(f32[8,6,1,1024]{3,2,0,1:T(1,128)S(1)} %copy.146), channel_id=1, source_target_pairs={{1,0},{2,1},{3,2},{4,3},{5,4},{6,5},{7,6},{8,7},{9,8},{10,9},{11,1... | collective-permute-start | bytes 589832 | tf_op jit(solution)/shard_map/ppermute | solution.py:22
where the time goes:
time: 111 us
  starting transfers between devices  38.1 us (34%)
  blocking collectives  31.4 us (28%)
  waiting for transfers between devices  24.7 us (22%)
  local copies, waits for them, and re-layouts  8.99 us (8%)
  matrix products  4.33 us (4%)
  other arithmetic  2.84 us (3%)
    all_to_all x1, blocking collectives, shards(): lax.all_to_all(bundle, 'mode', split_axis=0, concat_axis=2, tiled=True)  31.4 us
    ppermute x1, starting transfers between devices, padded(): lax.ppermute(lax.slice_in_dim(block, 0, width, axis=dim), axis, backward)  18.7 us
    all_to_all x1, starting transfers between devices, shards(): lax.all_to_all(split_cells(velocity), 'mode', split_axis=2, concat_axis=0...  12.9 us
    all_to_all x1, waiting for transfers between devices, shards(): lax.all_to_all(split_cells(velocity), 'mode', split_axis=2, concat_axis=0...  10.8 us
    all_to_all x1, waiting for transfers between devices, shards(): lax.all_to_all(split_cells(vorticity), 'mode', split_axis=2, concat_axis=...  10.7 us
    all_to_all x1, starting transfers between devices, shards(): lax.all_to_all(split_cells(vorticity), 'mode', split_axis=2, concat_axis=...  4.64 us
    reshape x2, local copies, waits for them, and re-layouts, split_cells(): source_field.reshape(row_count, source_field.shape[1], group_count, piece...  2.59 us
    dot_general x1, matrix products, shards(): jnp.dot(flat_coupling, spin_flat, precision=lax.Precision.HIGHEST)  2.57 us
  transfers between devices with their start and end apart: 4, of which 4 were waited for; matrix products, arithmetic and copies ran while one was open for 1% of the time, Pallas kernels for 0%

commit v1 on v0

--- a/solution.py
+++ b/solution.py
@@ -115,23 +115,9 @@
     )
 
 
-def rim_dx(rimmed):
-    return 0.5 * (rimmed[:, 2:] - rimmed[:, :-2])
-
-
-def core_dy(rimmed):
-    return centred(rimmed[:, 1:-1], 2)
-
-
-def plane_laplace(rimmed):
-    inner = rimmed[:, 1:-1]
-    return (
-        rimmed[:, 2:]
-        + rimmed[:, :-2]
-        + jnp.roll(inner, -1, 2)
-        + jnp.roll(inner, 1, 2)
-        - 4.0 * inner
-    )
+def pack_rows(block):
+    lead = block.shape[0]
+    return block.reshape(lead, -1, 128)
 
 
 def shards(velocity, vorticity, viscosity):
@@ -139,50 +125,80 @@
     cell_count = velocity.shape[2]
     slab_rows = cell_count // NY
     group_count = lax.axis_size("mode")
-    piece_cells = cell_count // group_count
+    chunk = NY // group_count
     planes = row_count * group_count // MODES
     coupling = jnp.asarray(triple_table(MODES), dtype=jnp.float32)
     mixing = viscosity[0] * coupling[0] + viscosity[1] * coupling[1]
     flat_coupling = jnp.transpose(coupling, (0, 2, 1)).reshape(MODES * MODES, MODES)
     mixing_rows = jnp.transpose(mixing)
 
-    def split_cells(source_field):
-        return source_field.reshape(row_count, source_field.shape[1], group_count, piece_cells)
-
-    speed_modes = lax.all_to_all(
-        split_cells(velocity), "mode", split_axis=2, concat_axis=0, tiled=True
-    )
-    width_cells = speed_modes.shape[3]
-    speed_four = speed_modes.reshape(MODES, planes, 3, width_cells)
-    spin_flat = lax.all_to_all(
-        split_cells(vorticity), "mode", split_axis=2, concat_axis=0, tiled=True
-    ).reshape(MODES, planes * 3 * width_cells)
+    def windows(source_field):
+        main = source_field.reshape(row_count, 3, slab_rows, group_count, chunk)
+        left = jnp.roll(main[..., chunk - 1], 1, axis=3)[..., None]
+        right = jnp.roll(main[..., 0], -1, axis=3)[..., None]
+        return jnp.concatenate([left, main, right], axis=4)
+
+    both = jnp.stack([windows(velocity), windows(vorticity)], axis=0)
+    both = jnp.transpose(both, (4, 0, 1, 2, 3, 5))
+    wide = chunk + 2
+    arrived = lax.all_to_all(pack_rows(both), "mode", split_axis=0, concat_axis=0, tiled=True)
+    arrived = arrived.reshape(MODES, group_count // MODES, 2, row_count, 3, slab_rows, wide)
+    arrived = jnp.transpose(arrived, (2, 0, 1, 3, 4, 5, 6)).reshape(
+        2, MODES, planes, 3, slab_rows, wide
+    )
+    speed = arrived[0]
+    spin_flat = arrived[1].reshape(MODES, -1)
     mixed_spin = jnp.dot(flat_coupling, spin_flat, precision=lax.Precision.HIGHEST).reshape(
-        MODES, MODES, planes, 3, width_cells
-    )
-    flux_terms = jnp.sum(cross_along(speed_four[:, None], mixed_spin, 3), axis=0)
+        MODES, MODES, planes, 3, slab_rows, wide
+    )
+    flux = jnp.sum(cross_along(speed[:, None], mixed_spin, 3), axis=0)
     damped = jnp.dot(mixing_rows, spin_flat, precision=lax.Precision.HIGHEST).reshape(
-        MODES, planes, 3, width_cells
-    )
-    flux_terms, damped, width_cells = (flux_terms, damped, width_cells)
-    extra_first = -centred(flux_terms[:, :, 1], 1) + second_diff(damped[:, :, 0], 1)
-    extra_second = centred(flux_terms[:, :, 0], 1) + second_diff(damped[:, :, 1], 1)
-    extra_third = second_diff(damped[:, :, 2], 1)
-    extras = jnp.stack([extra_first, extra_second, extra_third], axis=2)
-    bundle = jnp.concatenate([flux_terms, damped, extras], axis=2).reshape(
-        MODES * planes, 9, 1, width_cells
-    )
-    returned = lax.all_to_all(bundle, "mode", split_axis=0, concat_axis=2, tiled=True)
-    returned = returned.reshape(row_count, 9, slab_rows, NY)
-    rimmed = padded(returned[:, :6], (("tile", 2),), 1)
-    flux_x = rimmed[:, 0]
-    flux_y = rimmed[:, 1]
-    flux_z = rimmed[:, 2]
-    rate_x = core_dy(flux_z) + returned[:, 6] + plane_laplace(rimmed[:, 3])
-    rate_y = -rim_dx(flux_z) + returned[:, 7] + plane_laplace(rimmed[:, 4])
-    rate_z = rim_dx(flux_y) - core_dy(flux_x) + returned[:, 8] + plane_laplace(rimmed[:, 5])
-    result = jnp.stack([rate_x, rate_y, rate_z], axis=1)
-    return result.reshape(row_count, 3, cell_count)
+        MODES, planes, 3, slab_rows, wide
+    )
+    fields = jnp.concatenate([flux, damped], axis=2)
+    count = lax.axis_size("tile")
+    forward = [(i, (i + 1) % count) for i in range(count)]
+    backward = [((i + 1) % count, i) for i in range(count)]
+    edge_shape = fields[:, :, :, 0].shape
+    low = lax.ppermute(fields[:, :, :, slab_rows - 1].reshape(-1, 128), "tile", forward)
+    high = lax.ppermute(fields[:, :, :, 0].reshape(-1, 128), "tile", backward)
+    rim = jnp.concatenate(
+        [low.reshape(edge_shape)[:, :, :, None], fields, high.reshape(edge_shape)[:, :, :, None]],
+        axis=3,
+    )
+
+    def core(f):
+        return f[:, :, 1:-1, 1:-1]
+
+    def d_y(f):
+        return 0.5 * (f[:, :, 1:-1, 2:] - f[:, :, 1:-1, :-2])
+
+    def d_x(f):
+        return 0.5 * (f[:, :, 2:, 1:-1] - f[:, :, :-2, 1:-1])
+
+    def d_z(f):
+        return centred(core(f), 1)
+
+    def laplace(f):
+        inner = core(f)
+        return (
+            second_diff(inner, 1)
+            + (f[:, :, 2:, 1:-1] + f[:, :, :-2, 1:-1] - 2.0 * inner)
+            + (f[:, :, 1:-1, 2:] + f[:, :, 1:-1, :-2] - 2.0 * inner)
+        )
+
+    flux_x = rim[:, :, 0]
+    flux_y = rim[:, :, 1]
+    flux_z = rim[:, :, 2]
+    rate_x = d_y(flux_z) - d_z(flux_y) + laplace(rim[:, :, 3])
+    rate_y = d_z(flux_x) - d_x(flux_z) + laplace(rim[:, :, 4])
+    rate_z = d_x(flux_y) - d_y(flux_x) + laplace(rim[:, :, 5])
+    rate = jnp.stack([rate_x, rate_y, rate_z], axis=2)
+    rate = rate.reshape(group_count, -1)
+    returned = lax.all_to_all(pack_rows(rate), "mode", split_axis=0, concat_axis=0, tiled=True)
+    returned = returned.reshape(group_count, row_count, 3, slab_rows, chunk)
+    returned = jnp.transpose(returned, (1, 2, 3, 0, 4))
+    return returned.reshape(row_count, 3, cell_count)
 
 
 def solution(mesh):

time: 111 us -> 129 us (1.16)
  local copies, waits for them, and re-layouts: 8.99 us -> 42.6 us
  starting transfers between devices: 38.1 us -> 26.1 us
  blocking collectives: 31.4 us -> 19.9 us
  other arithmetic: 2.84 us -> 10.8 us
  waiting for transfers between devices: 24.7 us -> 22.7 us
  matrix products: 4.33 us -> 6.06 us
    reshape x4 -> x7, local copies, waits for them, and re-layouts: 3.41 us -> 21.3 us  [the longest x1 12.6 us: shards(): jnp.dot(flat_coupling, spin_flat, precision=lax.Precision.HIGHEST)]
    all_to_all x1, blocking collectives: 31.4 us -> 19.9 us  [shards(): lax.all_to_all(pack_rows(rate), 'mode', split_axis=0, concat_axis=0, tile...]
    ppermute x2, starting transfers between devices: 20.6 us -> 13.2 us  [the longest x1 11.3 us: shards(): high = lax.ppermute(fields[:, :, :, 0].reshape(-1, 128), 'tile', backward)]
    slice x7 -> x19, local copies, waits for them, and re-layouts: 0.96 us -> 8.11 us  [the longest x6 4.28 us: windows(): left = jnp.roll(main[..., chunk - 1], 1, axis=3)[..., None]]
    all_to_all x2 -> x1, starting transfers between devices: 17.5 us -> 12.8 us  [shards(): lax.all_to_all(pack_rows(both), 'mode', split_axis=0, concat_axis=0, tile...]
    broadcast_in_dim x0 -> x4, local copies, waits for them, and re-layouts: none -> 4.38 us  [the longest x2 2.22 us: windows(): left = jnp.roll(main[..., chunk - 1], 1, axis=3)[..., None]]
    sub x1, other arithmetic: 0.5 us -> 4.07 us  [cross_along(): component(left_vec, 1) * component(right_vec, 2)]
    another operation x3 -> x9, local copies, waits for them, and re-layouts: 0.28 us -> 3.53 us  [the longest x1 1.45 us: shards(): spin_flat = arrived[1].reshape(MODES, -1)]
  transfers between devices with their start and end apart: 4 -> 3, of which waited for: 4 -> 3; matrix products, arithmetic and copies ran while one was open for 1% -> 1% of each run, Pallas kernels for 0% -> 0%
where the time goes in v1:
time: 129 us
  local copies, waits for them, and re-layouts  42.6 us (33%)
  starting transfers between devices  26.1 us (20%)
  waiting for transfers between devices  22.7 us (18%)
  blocking collectives  19.9 us (15%)
  other arithmetic  10.8 us (8%)
  matrix products  6.06 us (5%)
    all_to_all x1, waiting for transfers between devices, shards(): lax.all_to_all(pack_rows(both), 'mode', split_axis=0, concat_axis=0, tile...  20 us
    all_to_all x1, blocking collectives, shards(): lax.all_to_all(pack_rows(rate), 'mode', split_axis=0, concat_axis=0, tile...  19.9 us
    all_to_all x1, starting transfers between devices, shards(): lax.all_to_all(pack_rows(both), 'mode', split_axis=0, concat_axis=0, tile...  12.8 us
    reshape x1, local copies, waits for them, and re-layouts, shards(): jnp.dot(flat_coupling, spin_flat, precision=lax.Precision.HIGHEST)  12.6 us
    ppermute x1, starting transfers between devices, shards(): high = lax.ppermute(fields[:, :, :, 0].reshape(-1, 128), 'tile', backward)  11.3 us
    slice x6, local copies, waits for them, and re-layouts, windows(): left = jnp.roll(main[..., chunk - 1], 1, axis=3)[..., None]  4.28 us
    sub x1, other arithmetic, cross_along(): component(left_vec, 1) * component(right_vec, 2)  4.07 us
    dot_general x1, matrix products, shards(): jnp.dot(flat_coupling, spin_flat, precision=lax.Precision.HIGHEST)  3.65 us
  transfers between devices with their start and end apart: 3, of which 3 were waited for; matrix products, arithmetic and copies ran while one was open for 1% of the time, Pallas kernels for 0%

profile of v1, /device:TPU:8, one launch (start us, length us, event | category | flops | bytes accessed | tf_op | source)
XLA Modules:
  0.0 128.5 jit_solution(16976076400837059089)
XLA Ops:
  0.0 1.3 %reshape.36 = f32[8,3,4,16,64]{4,3,2,0,1:T(8,128)S(1)} reshape(f32[8,3,4096]{2,0,1:T(8,128)} %param.5) | data formatting | bytes 786432 | tf_op jit(solution)/shard_map/reshape | solution.py:136
  1.3 0.3 fusion.40
  1.6 0.6 copy.78
  2.3 0.1 maximum_bitcast_fusion.5
  2.4 0.6 copy.80
  3.1 0.6 copy.79
  3.8 0.1 maximum_bitcast_fusion.6
  3.9 0.6 copy.81
  4.5 0.3 reshape.35
  4.8 1.5 %fusion.39 = (f32[8,3,4,16,1]{4,3,2,0,1:T(8,128)}, f32[8,3,4,16,1]{4,3,2,0,1:T(8,128)}) fusion(f32[8,3,4,16,64]{4,3,2,0,1:T(8,128)S(1)} %reshape.35), kind=kLoop, calls=%fused_computation.81 | loop fusion | bytes 24576 | tf_op jit(solution)/shard_map/slice | solution.py:137
  6.3 1.7 %copy.74 = f32[8,3,4,16,1]{3,0,4,2,1:T(8,128)S(1)} copy(f32[8,3,4,16,1]{4,3,2,0,1:T(8,128)} %get-tuple-element.21) | data formatting | bytes 12288 | tf_op jit(solution)/shard_map/slice | solution.py:137
  8.0 0.1 slice.339
  8.1 0.1 maximum_bitcast_fusion.3
  8.2 1.6 %copy.76 = f32[8,3,4,16,1]{4,3,2,0,1:T(8,128)} copy(f32[8,3,4,16,1]{3,0,4,2,1:T(8,128)S(1)} %maximum_bitcast_fusion.3) | data formatting | bytes 12288 | tf_op jit(solution)/shard_map/broadcast_in_dim | solution.py:137
  9.8 1.7 %copy.75 = f32[8,3,4,16,1]{3,0,4,2,1:T(8,128)S(1)} copy(f32[8,3,4,16,1]{4,3,2,0,1:T(8,128)} %get-tuple-element.22) | data formatting | bytes 12288 | tf_op jit(solution)/shard_map/slice | solution.py:138
  11.5 0.1 slice.342
  11.6 0.1 maximum_bitcast_fusion.4
  11.7 1.5 %copy.77 = f32[8,3,4,16,1]{4,3,2,0,1:T(8,128)} copy(f32[8,3,4,16,1]{3,0,4,2,1:T(8,128)S(1)} %maximum_bitcast_fusion.4) | data formatting | bytes 12288 | tf_op jit(solution)/shard_map/broadcast_in_dim | solution.py:138
  13.2 2.2 %maximum_bitcast_fusion.1 = (f32[1,8,3,4,16,66]{5,4,3,1,2,0:T(8,128)S(1)}, f32[1,8,3,4,16,66]{5,4,3,1,2,0:T(8,128)S(1)}) fusion(f32[8,3,4,16,1]{4,3,2,0,1:T(8,128)} %copy.77, f32[8,3,4,16,64]{4,3,2,0,1:T(8,128)S(1)} %reshape.35, f32[8,3,4,16,1]{4,3,2,0,1:T(8,128)} %copy.76, f32[8,3,4,16,1]{4,3,2,0,1:T(8,128)S(1)} %copy.81, ...), kind=kLoop, calls=%fused_computation.6 | loop fusion | flops 405504 | bytes 1622016 | tf_op jit(solution)/shard_map/stack | solution.py:141
  15.5 0.1 maximum_bitcast_fusion
  15.6 0.6 copy.82
  16.2 2.9 %reshape.37 = f32[16,99,128]{2,1,0:T(8,128)} reshape(f32[16,2,8,3,4,66]{5,4,3,2,1,0:T(4,128)S(1)} %copy.82) | data formatting | bytes 1622016 | tf_op jit(solution)/shard_map/reshape | solution.py:120
  19.2 12.8 %all-to-all-start = ((f32[16,99,128]{2,1,0:T(8,128)}), f32[16,99,128]{2,1,0:T(8,128)S(1)}, u32[]{:S(2)}, u32[]{:S(2)}) async-start(f32[16,99,128]{2,1,0:T(8,128)} %reshape.37), calls=%async_computation | async-start | bytes 1703936 | tf_op jit(solution)/shard_map/all_to_all | solution.py:144
  32.0 0.6 fusion.51
  32.6 20.0 %all-to-all-done = f32[16,99,128]{2,1,0:T(8,128)S(1)} async-done(((f32[16,99,128]{2,1,0:T(8,128)}), f32[16,99,128]{2,1,0:T(8,128)S(1)}, u32[]{:S(2)}, u32[]{:S(2)}) %all-to-all-start) | async-done | bytes 811040 | tf_op jit(solution)/shard_map/all_to_all | solution.py:144
  52.6 2.8 %reshape.38 = f32[8,2,2,8,3,4,66]{6,5,4,3,2,1,0:T(4,128)S(1)} reshape(f32[16,99,128]{2,1,0:T(8,128)S(1)} %all-to-all-done) | data formatting | bytes 1622016 | tf_op jit(solution)/shard_map/reshape | solution.py:145
  55.4 0.3 fusion.38
  55.7 1.0 slice_bitcast_fusion.7
  56.7 1.5 %reshape_squeeze.9 = f32[8,12672]{1,0:T(8,128)} reshape(f32[1,8,2,8,3,4,66]{6,5,4,3,0,2,1:T(4,128)S(1)} %get-tuple-element.17) | data formatting | bytes 811008 | tf_op jit(solution)/shard_map/reshape;squeeze | solution.py:150
  58.2 3.6 %fusion.52 = f32[64,12672]{1,0:T(8,128)S(1)} fusion(f32[64,8]{1,0:T(8,128)S(1)} %copy-done.2, f32[8,12672]{1,0:T(8,128)} %reshape_squeeze.9), kind=kOutput, calls=%fused_computation.94 | convolution fusion | flops 77856768 | bytes 3651584 | tf_op jit(solution)/shard_map/dot_general | solution.py:151
  61.8 12.6 %reshape.40 = f32[8,8,16,3,4,66]{5,4,3,2,1,0:T(4,128)} reshape(f32[64,12672]{1,0:T(8,128)S(1)} %fusion.52) | data formatting | bytes 6488064 | tf_op jit(solution)/shard_map/reshape | solution.py:151
  74.5 4.1 %multiply_subtract_fusion.2 = (f32[8,8,16,1,4,66]{5,4,3,2,1,0:T(4,128)S(1)}, f32[8,8,16,1,4,66]{5,4,3,2,1,0:T(4,128)S(1)}, f32[8,8,16,1,4,66]{5,4,3,2,1,0:T(4,128)S(1)}) fusion(f32[8,8,16,3,4,66]{5,4,3,2,1,0:T(4,128)} %reshape.40, f32[8,16,4,66]{3,2,1,0:T(4,128)S(1)} %get-tuple-element.18, f32[8,16,4,66]{3,2,1,0:T(4,128)} %get-tuple-element.20, ...), kind=kLoop, calls=%fused_computation.4 | loop fusion | flops 2433024 | bytes 6893568 | tf_op jit(solution)/shard_map/sub | solution.py:96
  78.5 2.2 %maximum_reduce_fusion = f32[8,16,3,4,66]{4,3,2,1,0:T(4,128)S(1)} fusion(f32[8,8,16,1,4,66]{5,4,3,2,1,0:T(4,128)S(1)} %get-tuple-element.7, f32[8,8,16,1,4,66]{5,4,3,2,1,0:T(4,128)S(1)} %get-tuple-element.6, f32[8,8,16,1,4,66]{5,4,3,2,1,0:T(4,128)S(1)} %get-tuple-element.5), kind=kLoop, calls=%fused_computation | loop fusion | flops 2331648 | bytes 3649536 | tf_op jit(solution)/shard_map/reduce_sum | solution.py:154
  80.8 0.5 copy.85
  81.2 1.3 %dot_general.15 = f32[16,3,4,66,8]{3,2,1,0,4:T(4,128)S(1)} reshape(f32[12672,8]{0,1:T(8,128)S(1)} %bitcast.86) | data formatting | bytes 811008 | tf_op jit(solution)/shard_map/dot_general | solution.py:155
  82.6 2.4 %fusion = f32[8,16,3,4,66]{4,0,3,2,1:T(8,128)S(1)} fusion(f32[16,3,4,66,8]{3,2,1,0,4:T(4,128)S(1)} %dot_general.15, f32[1,8,8]{2,1,0:T(8,128)S(1)} %copy-done.4, f32[1,8,8]{2,1,0:T(8,128)S(1)} %copy-done.3, f32[]{:T(128)} %bitcast.17, f32[]{:T(128)} %bitcast.16), kind=kOutput, calls=%fused_computation.9 | convolution fusion | flops 9732288 | bytes 811528 | tf_op jit(solution)/shard_map/dot_general | solution.py:155
  85.1 0.1 copy.86
  85.2 0.2 reshape_squeeze.10
  85.4 1.9 %collective-permute-start = (f32[396,128]{1,0:T(8,128)S(1)}, f32[396,128]{1,0:T(8,128)S(1)}, u32[]{:S(2)}, u32[]{:S(2)}) collective-permute-start(f32[396,128]{1,0:T(8,128)S(1)} %reshape_squeeze.10), channel_id=1, source_target_pairs={{0,1},{1,2},{2,3},{3,4},{4,5},{5,6},{6,7},{7,8},{8,9},{9,10},{10,1... | collective-permute-start | bytes 608264 | tf_op jit(solution)/shard_map/ppermute | solution.py:163
  87.3 0.1 copy.87
  87.4 0.2 reshape_squeeze.11
  87.7 11.3 %collective-permute-start.1 = (f32[396,128]{1,0:T(8,128)S(1)}, f32[396,128]{1,0:T(8,128)S(1)}, u32[]{:S(2)}, u32[]{:S(2)}) collective-permute-start(f32[396,128]{1,0:T(8,128)S(1)} %reshape_squeeze.11), channel_id=1, source_target_pairs={{1,0},{2,1},{3,2},{4,3},{5,4},{6,5},{7,6},{8,7},{9,8},{10,9},{11,1... | collective-permute-start | bytes 608264 | tf_op jit(solution)/shard_map/ppermute | solution.py:164
  99.0 1.2 collective-permute-done
  100.2 0.3 broadcast_in_dim_reshape.6
  100.5 0.2 copy.88
  100.7 1.6 %collective-permute-done.1 = f32[396,128]{1,0:T(8,128)S(1)} collective-permute-done((f32[396,128]{1,0:T(8,128)S(1)}, f32[396,128]{1,0:T(8,128)S(1)}, u32[]{:S(2)}, u32[]{:S(2)}) %collective-permute-start.1) | collective-permute-done | bytes 202784 | tf_op jit(solution)/shard_map/ppermute | solution.py:164
  102.3 0.3 broadcast_in_dim_reshape.7
  102.6 0.2 copy.89
  102.8 0.2 pad_maximum_fusion
  103.0 0.2 slice_bitcast_fusion.3
  103.2 0.2 fusion.42
  103.5 0.2 fusion.44
  103.8 0.2 fusion.46
  104.1 0.2 fusion.48
  104.3 0.2 fusion.50
  104.6 0.6 fusion.5
  105.2 0.4 fusion.22
  105.6 0.5 fusion.14
  106.1 0.2 copy.95
  106.4 0.4 reshape_reshape.3
  106.8 19.9 %all_to_all.10 = f32[16,48,128]{2,1,0:T(8,128)S(1)} all-to-all(f32[16,48,128]{2,1,0:T(8,128)S(1)} %reshape_reshape.3), channel_id=1, replica_groups=mesh['mode'=16,'tile'=48] {'mode'}, dimensions={0} | all-to-all | bytes 786432 | tf_op jit(solution)/shard_map/all_to_all | solution.py:198
  126.7 0.4 reshape.41
  127.0 0.5 copy.96
  127.5 1.0 reshape.42
  (21 shorter events, 0.7 us)
Async XLA Ops:
  1.6 2.9 %copy-start.1 = (f32[8,3,4096]{2,0,1:T(8,128)S(1)}, f32[8,3,4096]{2,0,1:T(8,128)}, u32[]{:S(2)}) copy-start(f32[8,3,4096]{2,0,1:T(8,128)} %param.4) | copy-start | bytes 1179652
  16.2 15.8 %copy-start.5 = (f32[2]{0:T(128)S(1)}, f32[2]{0:T(128)}, u32[]{:S(2)}) copy-start(f32[2]{0:T(128)} %param.6) | copy-start | bytes 28
  19.2 33.5 %all-to-all-start = ((f32[16,99,128]{2,1,0:T(8,128)}), f32[16,99,128]{2,1,0:T(8,128)S(1)}, u32[]{:S(2)}, u32[]{:S(2)}) async-start(f32[16,99,128]{2,1,0:T(8,128)} %reshape.37), calls=%async_computation | async-start | bytes 1703936 | tf_op jit(solution)/shard_map/all_to_all | solution.py:144
  55.7 2.5 %copy-start.2 = (f32[64,8]{1,0:T(8,128)S(1)}, f32[64,8]{1,0:T(8,128)}, u32[]{:S(2)}) copy-start(f32[64,8]{1,0:T(8,128)} %constant.12) | copy-start | bytes 6148
  78.5 2.7 %copy-start = (f32[8,12672]{1,0:T(8,128)S(1)}, f32[8,12672]{1,0:T(8,128)}, u32[]{:S(2)}) copy-start(f32[8,12672]{1,0:T(8,128)} %reshape_squeeze.9) | copy-start | bytes 1216516
  80.7 1.8 %copy-start.3 = (f32[1,8,8]{2,1,0:T(8,128)S(1)}, f32[1,8,8]{2,1,0:T(8,128)}, u32[]{:S(2)}) copy-start(f32[1,8,8]{2,1,0:T(8,128)} %constant.13) | copy-start | bytes 772
  80.8 1.8 %copy-start.4 = (f32[1,8,8]{2,1,0:T(8,128)S(1)}, f32[1,8,8]{2,1,0:T(8,128)}, u32[]{:S(2)}) copy-start(f32[1,8,8]{2,1,0:T(8,128)} %constant.14) | copy-start | bytes 772
  85.4 14.8 %collective-permute-start = (f32[396,128]{1,0:T(8,128)S(1)}, f32[396,128]{1,0:T(8,128)S(1)}, u32[]{:S(2)}, u32[]{:S(2)}) collective-permute-start(f32[396,128]{1,0:T(8,128)S(1)} %reshape_squeeze.10), channel_id=1, source_target_pairs={{0,1},{1,2},{2,3},{3,4},{4,5},{5,6},{6,7},{7,8},{8,9},{9,10},{10,1... | collective-permute-start | bytes 608264 | tf_op jit(solution)/shard_map/ppermute | solution.py:163
  87.7 14.6 %collective-permute-start.1 = (f32[396,128]{1,0:T(8,128)S(1)}, f32[396,128]{1,0:T(8,128)S(1)}, u32[]{:S(2)}, u32[]{:S(2)}) collective-permute-start(f32[396,128]{1,0:T(8,128)S(1)} %reshape_squeeze.11), channel_id=1, source_target_pairs={{1,0},{2,1},{3,2},{4,3},{5,4},{6,5},{7,6},{8,7},{9,8},{10,9},{11,1... | collective-permute-start | bytes 608264 | tf_op jit(solution)/shard_map/ppermute | solution.py:164

commit v2 on v0

--- a/solution.py
+++ b/solution.py
@@ -1,9 +1,12 @@
+import functools
 import math
 
 import jax
 import jax.numpy as jnp
 import numpy as np
 from jax import lax
+from jax.experimental import pallas as pl
+from jax.experimental.pallas import tpu as pltpu
 from jax.sharding import PartitionSpec as P
 
 MODES = 8
@@ -115,23 +118,46 @@
     )
 
 
-def rim_dx(rimmed):
-    return 0.5 * (rimmed[:, 2:] - rimmed[:, :-2])
-
-
-def core_dy(rimmed):
-    return centred(rimmed[:, 1:-1], 2)
-
-
-def plane_laplace(rimmed):
-    inner = rimmed[:, 1:-1]
-    return (
-        rimmed[:, 2:]
-        + rimmed[:, :-2]
-        + jnp.roll(inner, -1, 2)
-        + jnp.roll(inner, 1, 2)
-        - 4.0 * inner
-    )
+def stencil_kernel(chunk, slab_rows, f_ref, r_ref, lo_ref, hi_ref, o_ref):
+    planes, piece = f_ref.shape[2], f_ref.shape[3]
+    lane = lax.broadcasted_iota(jnp.int32, (planes, piece), 1)
+    y_of = lane % chunk
+    x_of = lane // chunk
+    first_y = y_of == 0
+    last_y = y_of == chunk - 1
+    first_x = x_of == 0
+    last_x = x_of == slab_rows - 1
+
+    for k in range(f_ref.shape[1]):
+
+        def rim(c, side):
+            out = jnp.zeros((planes, piece), jnp.float32)
+            for row in range(slab_rows):
+                out = jnp.where(x_of == row, r_ref[c, k, side, row], out)
+            return out
+
+        def moved(c, halo):
+            f = f_ref[c, k]
+            y_up = jnp.where(last_y, rim(c, 1), pltpu.roll(f, piece - 1, 1))
+            y_down = jnp.where(first_y, rim(c, 0), pltpu.roll(f, 1, 1))
+            z_up = pltpu.roll(f, planes - 1, 0)
+            z_down = pltpu.roll(f, 1, 0)
+            if halo is None:
+                return f, y_up, y_down, z_up, z_down, None, None
+            x_up = jnp.where(last_x, hi_ref[halo, k], pltpu.roll(f, piece - chunk, 1))
+            x_down = jnp.where(first_x, lo_ref[halo, k], pltpu.roll(f, chunk, 1))
+            return f, y_up, y_down, z_up, z_down, x_up, x_down
+
+        def laplace(c):
+            f, y_up, y_down, z_up, z_down, x_up, x_down = moved(3 + c, 2 + c)
+            return (z_up + z_down - 2.0 * f) + (x_up + x_down - 2.0 * f) + (y_up + y_down - 2.0 * f)
+
+        _, fx_yu, fx_yd, fx_zu, fx_zd, _, _ = moved(0, None)
+        _, fy_yu, fy_yd, fy_zu, fy_zd, fy_xu, fy_xd = moved(1, 0)
+        _, fz_yu, fz_yd, fz_zu, fz_zd, fz_xu, fz_xd = moved(2, 1)
+        o_ref[k, 0] = 0.5 * (fz_yu - fz_yd) - 0.5 * (fy_zu - fy_zd) + laplace(0)
+        o_ref[k, 1] = 0.5 * (fx_zu - fx_zd) - 0.5 * (fz_xu - fz_xd) + laplace(1)
+        o_ref[k, 2] = 0.5 * (fy_xu - fy_xd) - 0.5 * (fx_yu - fx_yd) + laplace(2)
 
 
 def shards(velocity, vorticity, viscosity):
@@ -139,50 +165,86 @@
     cell_count = velocity.shape[2]
     slab_rows = cell_count // NY
     group_count = lax.axis_size("mode")
-    piece_cells = cell_count // group_count
-    planes = row_count * group_count // MODES
+    chunk = NY // group_count
+    piece = slab_rows * chunk
+    halves = group_count // MODES
+    planes = row_count * halves
     coupling = jnp.asarray(triple_table(MODES), dtype=jnp.float32)
     mixing = viscosity[0] * coupling[0] + viscosity[1] * coupling[1]
     flat_coupling = jnp.transpose(coupling, (0, 2, 1)).reshape(MODES * MODES, MODES)
     mixing_rows = jnp.transpose(mixing)
 
-    def split_cells(source_field):
-        return source_field.reshape(row_count, source_field.shape[1], group_count, piece_cells)
-
-    speed_modes = lax.all_to_all(
-        split_cells(velocity), "mode", split_axis=2, concat_axis=0, tiled=True
+    both = jnp.stack([velocity, vorticity], axis=0).reshape(
+        2, row_count, 3, slab_rows, group_count, chunk
     )
-    width_cells = speed_modes.shape[3]
-    speed_four = speed_modes.reshape(MODES, planes, 3, width_cells)
-    spin_flat = lax.all_to_all(
-        split_cells(vorticity), "mode", split_axis=2, concat_axis=0, tiled=True
-    ).reshape(MODES, planes * 3 * width_cells)
-    mixed_spin = jnp.dot(flat_coupling, spin_flat, precision=lax.Precision.HIGHEST).reshape(
-        MODES, MODES, planes, 3, width_cells
-    )
-    flux_terms = jnp.sum(cross_along(speed_four[:, None], mixed_spin, 3), axis=0)
-    damped = jnp.dot(mixing_rows, spin_flat, precision=lax.Precision.HIGHEST).reshape(
-        MODES, planes, 3, width_cells
-    )
-    flux_terms, damped, width_cells = (flux_terms, damped, width_cells)
-    extra_first = -centred(flux_terms[:, :, 1], 1) + second_diff(damped[:, :, 0], 1)
-    extra_second = centred(flux_terms[:, :, 0], 1) + second_diff(damped[:, :, 1], 1)
-    extra_third = second_diff(damped[:, :, 2], 1)
-    extras = jnp.stack([extra_first, extra_second, extra_third], axis=2)
-    bundle = jnp.concatenate([flux_terms, damped, extras], axis=2).reshape(
-        MODES * planes, 9, 1, width_cells
-    )
-    returned = lax.all_to_all(bundle, "mode", split_axis=0, concat_axis=2, tiled=True)
-    returned = returned.reshape(row_count, 9, slab_rows, NY)
-    rimmed = padded(returned[:, :6], (("tile", 2),), 1)
-    flux_x = rimmed[:, 0]
-    flux_y = rimmed[:, 1]
-    flux_z = rimmed[:, 2]
-    rate_x = core_dy(flux_z) + returned[:, 6] + plane_laplace(rimmed[:, 3])
-    rate_y = -rim_dx(flux_z) + returned[:, 7] + plane_laplace(rimmed[:, 4])
-    rate_z = rim_dx(flux_y) - core_dy(flux_x) + returned[:, 8] + plane_laplace(rimmed[:, 5])
-    result = jnp.stack([rate_x, rate_y, rate_z], axis=1)
-    return result.reshape(row_count, 3, cell_count)
+    main = jnp.transpose(both, (4, 0, 2, 1, 3, 5)).reshape(group_count, -1)
+    left = jnp.roll(both[..., chunk - 1], 1, axis=4)
+    right = jnp.roll(both[..., 0], -1, axis=4)
+    rims = jnp.stack([left, right], axis=-1)
+    rims = jnp.transpose(rims, (4, 0, 2, 1, 3, 5)).reshape(group_count, -1)
+    main_len = main.shape[1]
+    sent = jnp.concatenate([main, rims], axis=1).reshape(group_count, -1, 128)
+    arrived = lax.all_to_all(sent, "mode", split_axis=0, concat_axis=0, tiled=True)
+    arrived = arrived.reshape(group_count, -1)
+    body = arrived[:, :main_len].reshape(MODES, halves, 2, 3, row_count, piece)
+    body = jnp.transpose(body, (2, 3, 0, 1, 4, 5)).reshape(2, 3, MODES, planes, piece)
+    edge = arrived[:, main_len:].reshape(MODES, halves, 2, 3, row_count, slab_rows, 2)
+    edge = jnp.transpose(edge, (2, 3, 0, 1, 4, 5, 6)).reshape(2, 3, MODES, planes, slab_rows, 2)
+
+    def coupled(speed, spin):
+        shape = spin.shape
+        mixed = [
+            jnp.dot(flat_coupling, spin[c].reshape(MODES, -1), precision=lax.Precision.HIGHEST)
+            .reshape((MODES, MODES) + shape[2:])
+            for c in range(3)
+        ]
+        flux = [
+            jnp.sum(speed[1][:, None] * mixed[2] - speed[2][:, None] * mixed[1], axis=0),
+            jnp.sum(speed[2][:, None] * mixed[0] - speed[0][:, None] * mixed[2], axis=0),
+            jnp.sum(speed[0][:, None] * mixed[1] - speed[1][:, None] * mixed[0], axis=0),
+        ]
+        damped = [
+            jnp.dot(mixing_rows, spin[c].reshape(MODES, -1), precision=lax.Precision.HIGHEST)
+            .reshape((MODES,) + shape[2:])
+            for c in range(3)
+        ]
+        return flux, damped
+
+    flux, damped = coupled(body[0], body[1])
+    flux_rim, damped_rim = coupled(edge[0], edge[1])
+
+    count = lax.axis_size("tile")
+    forward = [(i, (i + 1) % count) for i in range(count)]
+    backward = [((i + 1) % count, i) for i in range(count)]
+    x_needs = jnp.stack([flux[1], flux[2], damped[0], damped[1], damped[2]], axis=0)
+    x_shape = x_needs[..., :chunk].shape
+    low = lax.ppermute(x_needs[..., piece - chunk :].reshape(-1, 128), "tile", forward)
+    high = lax.ppermute(x_needs[..., :chunk].reshape(-1, 128), "tile", backward)
+    low = low.reshape(x_shape)
+    high = high.reshape(x_shape)
+
+    fields = jnp.stack(flux + damped, axis=0)
+    rims = jnp.stack(flux_rim + damped_rim, axis=0)
+    rims = jnp.transpose(rims, (0, 1, 4, 3, 2))[..., None]
+    low = jnp.tile(low, (1, 1, 1, slab_rows))
+    high = jnp.tile(high, (1, 1, 1, slab_rows))
+    rate = pl.pallas_call(
+        functools.partial(stencil_kernel, chunk, slab_rows),
+        out_shape=jax.ShapeDtypeStruct((MODES, 3, planes, piece), jnp.float32),
+        in_specs=[pl.BlockSpec(memory_space=pltpu.VMEM)] * 4,
+        out_specs=pl.BlockSpec(memory_space=pltpu.VMEM),
+        cost_estimate=pl.CostEstimate(
+            flops=MODES * 3 * planes * piece * 40,
+            bytes_accessed=(6 + 10 + 3) * MODES * planes * piece * 4,
+            transcendentals=0,
+        ),
+    )(fields, rims, low, high)
+    rate = rate.reshape(MODES, 3, halves, row_count, piece)
+    rate = jnp.transpose(rate, (0, 2, 1, 3, 4)).reshape(group_count, -1, 128)
+    returned = lax.all_to_all(rate, "mode", split_axis=0, concat_axis=0, tiled=True)
+    returned = returned.reshape(group_count, 3, row_count, slab_rows, chunk)
+    returned = jnp.transpose(returned, (2, 1, 3, 0, 4))
+    return returned.reshape(row_count, 3, cell_count)
 
 
 def solution(mesh):

time: 111 us -> 120 us (1.081)
  local copies, waits for them, and re-layouts: 8.99 us -> 33.1 us
  starting transfers between devices: 38.1 us -> 26.3 us
  blocking collectives: 31.4 us -> 19.9 us
  matrix products: 4.33 us -> 13.8 us
  waiting for transfers between devices: 24.7 us -> 20 us
  Pallas kernels: 0 us -> 4.48 us
  other arithmetic: 2.84 us -> 1.54 us
    all_to_all x1, blocking collectives: 31.4 us -> 19.9 us  [shards(): lax.all_to_all(rate, 'mode', split_axis=0, concat_axis=0, tiled=True)]
    dot_general x2 -> x12, matrix products: 4.33 us -> 13.8 us  [the longest x6 10.3 us: coupled(): jnp.dot(mixing_rows, spin[c].reshape(MODES, -1), precision=lax.Precision....]
    another operation x3 -> x10, local copies, waits for them, and re-layouts: 0.28 us -> 7.7 us  [the longest x3 2.96 us: shards(): high = jnp.tile(high, (1, 1, 1, slab_rows))]
    ppermute x2, starting transfers between devices: 20.6 us -> 13.4 us  [the longest x1 11.5 us: shards(): high = lax.ppermute(x_needs[..., :chunk].reshape(-1, 128), 'tile', backward)]
    slice x11 -> x12, local copies, waits for them, and re-layouts: 1.39 us -> 7.97 us  [the longest x3 4.89 us: shards(): left = jnp.roll(both[..., chunk - 1], 1, axis=4)]
    all_to_all x2 -> x1, starting transfers between devices: 17.5 us -> 12.8 us  [shards(): lax.all_to_all(sent, 'mode', split_axis=0, concat_axis=0, tiled=True)]
    reshape x4 -> x12, local copies, waits for them, and re-layouts: 3.41 us -> 7.98 us  [the longest x1 2.02 us: shards(): main = jnp.transpose(both, (4, 0, 2, 1, 3, 5)).reshape(group_count, -1)]
    pallas_call x0 -> x1, Pallas kernels: none -> 4.48 us  [shards(): pl.pallas_call(functools.partial(stencil_kernel, chunk, slab_rows), out_s...]
  transfers between devices with their start and end apart: 4 -> 3, of which waited for: 4 -> 1; matrix products, arithmetic and copies ran while one was open for 1% -> 17% of each run, Pallas kernels for 0% -> 0%
where the time goes in v2:
time: 120 us
  local copies, waits for them, and re-layouts  33.1 us (28%)
  starting transfers between devices  26.3 us (22%)
  waiting for transfers between devices  20 us (17%)
  blocking collectives  19.9 us (17%)
  matrix products  13.8 us (12%)
  Pallas kernels  4.48 us (4%)
  other arithmetic  1.54 us (1%)
    all_to_all x1, waiting for transfers between devices, shards(): lax.all_to_all(sent, 'mode', split_axis=0, concat_axis=0, tiled=True)  20 us
    all_to_all x1, blocking collectives, shards(): lax.all_to_all(rate, 'mode', split_axis=0, concat_axis=0, tiled=True)  19.9 us
    all_to_all x1, starting transfers between devices, shards(): lax.all_to_all(sent, 'mode', split_axis=0, concat_axis=0, tiled=True)  12.8 us
    ppermute x1, starting transfers between devices, shards(): high = lax.ppermute(x_needs[..., :chunk].reshape(-1, 128), 'tile', backward)  11.5 us
    dot_general x6, matrix products, coupled(): jnp.dot(mixing_rows, spin[c].reshape(MODES, -1), precision=lax.Precision....  10.3 us
    slice x3, local copies, waits for them, and re-layouts, shards(): left = jnp.roll(both[..., chunk - 1], 1, axis=4)  4.89 us
    pallas_call x1, Pallas kernels, shards(): pl.pallas_call(functools.partial(stencil_kernel, chunk, slab_rows), out_s...  4.48 us
    broadcast_in_dim x1, local copies, waits for them, and re-layouts, shards(): rims = jnp.transpose(rims, (0, 1, 4, 3, 2))[..., None]  3.56 us
  transfers between devices with their start and end apart: 3, of which 1 were waited for; matrix products, arithmetic and copies ran while one was open for 17% of the time, Pallas kernels for 0%

profile of v2, /device:TPU:8, one launch (start us, length us, event | category | flops | bytes accessed | tf_op | source)
XLA Modules:
  0.0 119.6 jit_solution(5160151563160760139)
XLA Ops:
  0.0 1.4 %stack.47 = f32[1,8,3,4,16,64]{5,4,3,1,2,0:T(8,128)S(1)} reshape(f32[8,3,4096]{2,0,1:T(8,128)} %param.4) | data formatting | bytes 786432 | tf_op jit(solution)/shard_map/stack | solution.py:177
  1.5 0.3 stack.48
  1.9 2.2 %fusion.28 = (f32[2,8,3,4,16,1]{5,4,3,1,2,0:T(8,128)}, f32[2,8,3,4,16,1]{5,4,3,1,2,0:T(8,128)}) fusion(f32[2,8,3,4,16,64]{5,4,3,1,2,0:T(8,128)S(1)} %constant_dynamic-update-slice_fusion), kind=kLoop, calls=%fused_computation.66 | loop fusion | bytes 49152 | tf_op jit(solution)/shard_map/slice | solution.py:181
  4.1 0.6 copy.106
  4.7 2.0 %reshape.146 = f32[16,12288]{1,0:T(8,128)} reshape(f32[16,2,3,8,4,64]{5,4,3,2,1,0:T(4,128)S(1)} %copy.106) | data formatting | bytes 1572864 | tf_op jit(solution)/shard_map/reshape | solution.py:180
  6.7 2.6 %copy.107 = f32[2,8,3,4,16,1]{4,1,5,3,2,0:T(8,128)S(1)} copy(f32[2,8,3,4,16,1]{5,4,3,1,2,0:T(8,128)} %get-tuple-element.17) | data formatting | bytes 24576 | tf_op jit(solution)/shard_map/slice | solution.py:181
  9.3 0.1 slice.153
  9.4 1.2 copy.108
  10.6 0.1 slice.156
  10.7 0.1 maximum_bitcast_fusion.1
  10.9 0.2 copy.109
  11.2 1.0 reshape.148
  12.2 12.8 %all-to-all-start = ((f32[16,99,128]{2,1,0:T(8,128)}), f32[16,99,128]{2,1,0:T(8,128)S(1)}, u32[]{:S(2)}, u32[]{:S(2)}) async-start(f32[16,99,128]{2,1,0:T(8,128)} %reshape.148), calls=%async_computation | async-start | bytes 1703936 | tf_op jit(solution)/shard_map/all_to_all | solution.py:187
  25.1 0.6 fusion.30
  25.7 20.0 %all-to-all-done = f32[16,99,128]{2,1,0:T(8,128)S(1)} async-done(((f32[16,99,128]{2,1,0:T(8,128)}), f32[16,99,128]{2,1,0:T(8,128)S(1)}, u32[]{:S(2)}, u32[]{:S(2)}) %all-to-all-start) | async-done | bytes 811040 | tf_op jit(solution)/shard_map/all_to_all | solution.py:187
  45.7 0.2 copy.195
  45.9 0.2 copy.160
  46.4 0.3 copy-done.5
  46.6 1.6 %fusion.9 = f32[8,16,256]{2,0,1:T(8,128)S(1)} fusion(f32[1,8,8]{2,1,0:T(8,128)S(1)} %copy-done.5, f32[1,8,8]{2,1,0:T(8,128)S(1)} %copy-done.6, f32[]{:T(128)} %bitcast.18, f32[]{:T(128)} %bitcast.17, f32[1,8,16,256]{3,2,1,0:T(8,128)S(1)} %get-tuple-element.19), kind=kOutput, calls=%fused_computation.46 | convolution fusion | flops 3145920 | bytes 262664 | tf_op jit(solution)/shard_map/dot_general | solution.py:207
  48.2 1.6 %fusion.13 = f32[8,16,256]{2,0,1:T(8,128)S(1)} fusion(f32[1,8,8]{2,1,0:T(8,128)S(1)} %copy-done.5, f32[1,8,8]{2,1,0:T(8,128)S(1)} %copy-done.6, f32[]{:T(128)} %bitcast.18, f32[]{:T(128)} %bitcast.17, f32[1,8,16,256]{3,2,1,0:T(8,128)S(1)} %get-tuple-element.21), kind=kOutput, calls=%fused_computation.50 | convolution fusion | flops 3145920 | bytes 262664 | tf_op jit(solution)/shard_map/dot_general | solution.py:207
  49.9 1.6 %fusion.11 = f32[8,16,256]{2,0,1:T(8,128)S(1)} fusion(f32[1,8,8]{2,1,0:T(8,128)S(1)} %copy-done.5, f32[1,8,8]{2,1,0:T(8,128)S(1)} %copy-done.6, f32[]{:T(128)} %bitcast.18, f32[]{:T(128)} %bitcast.17, f32[1,8,16,256]{3,2,1,0:T(8,128)S(1)} %get-tuple-element.22), kind=kOutput, calls=%fused_computation.48 | convolution fusion | flops 3145920 | bytes 262664 | tf_op jit(solution)/shard_map/dot_general | solution.py:207
  51.6 0.9 fusion.38
  52.5 0.9 fusion.39
  53.5 0.9 fusion.37
  54.4 0.6 subtract_reduce_fusion
  55.3 0.2 fusion.29
  55.5 0.8 reshape.160
  56.3 0.1 reshape.159
  56.4 1.9 %collective-permute-start = (f32[320,128]{1,0:T(8,128)S(1)}, f32[320,128]{1,0:T(8,128)}, u32[]{:S(2)}, u32[]{:S(2)}) collective-permute-start(f32[320,128]{1,0:T(8,128)S(1)} %reshape.159), channel_id=1, source_target_pairs={{0,1},{1,2},{2,3},{3,4},{4,5},{5,6},{6,7},{7,8},{8,9},{9,10},{10,1... | collective-permute-start | bytes 491528 | tf_op jit(solution)/shard_map/ppermute | solution.py:221
  58.3 11.5 %collective-permute-start.1 = (f32[320,128]{1,0:T(8,128)}, f32[320,128]{1,0:T(8,128)}, u32[]{:S(2)}, u32[]{:S(2)}) collective-permute-start(f32[320,128]{1,0:T(8,128)} %reshape.160), channel_id=1, source_target_pairs={{1,0},{2,1},{3,2},{4,3},{5,4},{6,5},{7,6},{8,7},{9,8},{10,9},{11,1... | collective-permute-start | bytes 491528 | tf_op jit(solution)/shard_map/ppermute | solution.py:222
  69.8 2.0 %reshape.155 = f32[8,2,2,3,8,4,2]{6,5,4,3,2,1,0:T(4,128)S(1)} reshape(f32[16,384]{1,0:T(8,128)S(1)} %slice.165) | data formatting | bytes 49152 | tf_op jit(solution)/shard_map/reshape | solution.py:191
  71.8 0.2 fusion.27
  72.0 0.5 copy.121
  72.5 0.5 copy.129
  73.0 0.5 copy.127
  73.5 0.5 copy.124
  73.9 0.2 fusion.41
  74.1 0.2 fusion.42
  74.4 0.2 fusion.40
  74.6 0.5 copy.123
  75.0 0.5 copy.120
  75.5 0.2 reshape.156
  75.7 0.2 reshape.158
  75.9 0.2 reshape.157
  76.1 0.7 subtract_reduce_fusion.3
  76.8 0.1 copy.131
  76.9 0.1 copy.126
  77.0 0.1 copy.130
  77.1 1.9 %fusion.2 = f32[6,8,16,4,2]{2,1,4,3,0:T(8,128)S(1)} fusion(f32[6,8,16,4,2]{2,1,4,3,0:T(8,128)S(1)} %constant_dynamic-update-slice_fusion.2, f32[16,4,2,8]{3,2,1,0:T(2,128)S(1)} %bitcast.205, f32[1,8,8]{2,1,0:T(8,128)S(1)} %copy-done.5, f32[1,8,8]{2,1,0:T(8,128)S(1)} %copy-done.6, f32[]{:T(128)} %bitcast.18, f32[]{:T(128)} %bitcast.17), kind=kOutput, calls=%fused_computation.5 | convolution fusion | flops 98496 | bytes 106504 | tf_op jit(solution)/shard_map/dot_general | solution.py:207
  79.0 1.9 %fusion.1 = f32[6,8,16,4,2]{2,1,4,3,0:T(8,128)S(1)} fusion(f32[6,8,16,4,2]{2,1,4,3,0:T(8,128)S(1)} %fusion.2, f32[16,4,2,8]{3,2,1,0:T(2,128)S(1)} %bitcast.203, f32[1,8,8]{2,1,0:T(8,128)S(1)} %copy-done.5, f32[1,8,8]{2,1,0:T(8,128)S(1)} %copy-done.6, f32[]{:T(128)} %bitcast.18, f32[]{:T(128)} %bitcast.17), kind=kOutput, calls=%fused_computation.3 | convolution fusion | flops 98496 | bytes 106504 | tf_op jit(solution)/shard_map/dot_general | solution.py:207
  80.9 1.9 %fusion = f32[6,8,16,4,2]{2,1,4,3,0:T(8,128)S(1)} fusion(f32[6,8,16,4,2]{2,1,4,3,0:T(8,128)S(1)} %fusion.1, f32[16,4,2,8]{3,2,1,0:T(2,128)S(1)} %bitcast.201, f32[1,8,8]{2,1,0:T(8,128)S(1)} %copy-done.5, f32[1,8,8]{2,1,0:T(8,128)S(1)} %copy-done.6, f32[]{:T(128)} %bitcast.18, f32[]{:T(128)} %bitcast.17), kind=kOutput, calls=%fused_computation.1 | convolution fusion | flops 98496 | bytes 106504 | tf_op jit(solution)/shard_map/dot_general | solution.py:207
  82.7 3.6 %copy.139.r_ref = f32[6,8,2,4,16,1]{5,4,3,2,1,0:T(8,128)} copy(f32[6,8,2,4,16,1]{4,1,2,3,0,5:T(8,128)S(1)} %bitcast.209) | data formatting | bytes 49152 | tf_op jit(solution)/shard_map/broadcast_in_dim | solution.py:228
  86.3 1.0 tile.23
  87.3 0.3 tile.24
  87.7 1.6 %tile.25.hi_ref = f32[5,8,16,256]{3,2,1,0:T(8,128)} reshape(f32[5,8,16,4,64]{4,3,2,1,0:T(4,128)S(1)} %tile.24) | data formatting | bytes 1310720 | tf_op jit(solution)/shard_map/tile | solution.py:230
  89.3 1.0 tile.20
  90.3 0.3 tile.21
  90.7 1.6 %tile.22.lo_ref = f32[5,8,16,256]{3,2,1,0:T(8,128)} reshape(f32[5,8,16,4,64]{4,3,2,1,0:T(4,128)S(1)} %tile.21) | data formatting | bytes 1310720 | tf_op jit(solution)/shard_map/tile | solution.py:229
  92.2 4.5 %shard_map.46 = f32[8,3,16,256]{3,2,1,0:T(8,128)} custom-call(f32[6,8,16,256]{3,2,1,0:T(8,128)} %copy-done.3, f32[6,8,2,4,16,1]{5,4,3,2,1,0:T(8,128)} %copy.139.r_ref, f32[5,8,16,256]{3,2,1,0:T(8,128)} %tile.22.lo_ref, f32[5,8,16,256]{3,2,1,0:T(8,128)} %tile.25.hi_ref), custom_call_target="tpu_custom_call" | custom-call | flops 3932160 | bytes 2490368 | tf_op jit(solution)/shard_map/pallas_call | solution.py:231
  96.7 1.0 copy_bitcast_fusion.1
  97.8 19.9 %all_to_all.10 = f32[16,48,128]{2,1,0:T(8,128)S(1)} all-to-all(f32[16,48,128]{2,1,0:T(8,128)S(1)} %reshape.162), channel_id=1, replica_groups=mesh['mode'=16,'tile'=48] {'mode'}, dimensions={0} | all-to-all | bytes 786432 | tf_op jit(solution)/shard_map/all_to_all | solution.py:244
  117.7 0.4 reshape.163
  118.1 0.5 copy.141
  118.5 1.0 reshape.164
  (38 shorter events, 1.1 us)
Async XLA Ops:
  0.0 1.4 %copy-start.4 = (f32[8,3,4096]{2,0,1:T(8,128)S(1)}, f32[8,3,4096]{2,0,1:T(8,128)}, u32[]{:S(2)}) copy-start(f32[8,3,4096]{2,0,1:T(8,128)} %param.5) | copy-start | bytes 1179652
  4.7 4.7 %copy-start = (f32[2,8,3,4,16,1]{5,4,3,1,2,0:T(8,128)S(1)}, f32[2,8,3,4,16,1]{5,4,3,1,2,0:T(8,128)}, u32[]{:S(2)}) copy-start(f32[2,8,3,4,16,1]{5,4,3,1,2,0:T(8,128)} %get-tuple-element.18) | copy-start | bytes 36868
  9.4 1.7 %copy-start.1 = (f32[16,12288]{1,0:T(8,128)S(1)}, f32[16,12288]{1,0:T(8,128)}, u32[]{:S(2)}) copy-start(f32[16,12288]{1,0:T(8,128)} %reshape.146) | copy-start | bytes 2359300
  11.2 13.9 %copy-start.7 = (f32[2]{0:T(128)S(1)}, f32[2]{0:T(128)}, u32[]{:S(2)}) copy-start(f32[2]{0:T(128)} %param.6) | copy-start | bytes 28
  12.2 33.5 %all-to-all-start = ((f32[16,99,128]{2,1,0:T(8,128)}), f32[16,99,128]{2,1,0:T(8,128)S(1)}, u32[]{:S(2)}, u32[]{:S(2)}) async-start(f32[16,99,128]{2,1,0:T(8,128)} %reshape.148), calls=%async_computation | async-start | bytes 1703936 | tf_op jit(solution)/shard_map/all_to_all | solution.py:187
  45.9 0.7 copy-start.5
  45.9 0.7 copy-start.6
  46.2 5.4 %copy-start.2 = (f32[64,8]{1,0:T(8,128)S(1)}, f32[64,8]{1,0:T(8,128)}, u32[]{:S(2)}) copy-start(f32[64,8]{1,0:T(8,128)} %constant.8) | copy-start | bytes 6148
  55.3 16.5 %copy-start.3 = (f32[6,8,16,256]{3,2,1,0:T(8,128)}, f32[6,8,16,256]{3,2,1,0:T(8,128)S(1)}, u32[]{:S(2)}) copy-start(f32[6,8,16,256]{3,2,1,0:T(8,128)S(1)} %get-tuple-element.28.f_ref) | copy-start | bytes 2359300
  56.4 32.9 %collective-permute-start = (f32[320,128]{1,0:T(8,128)S(1)}, f32[320,128]{1,0:T(8,128)}, u32[]{:S(2)}, u32[]{:S(2)}) collective-permute-start(f32[320,128]{1,0:T(8,128)S(1)} %reshape.159), channel_id=1, source_target_pairs={{0,1},{1,2},{2,3},{3,4},{4,5},{5,6},{6,7},{7,8},{8,9},{9,10},{10,1... | collective-permute-start | bytes 491528 | tf_op jit(solution)/shard_map/ppermute | solution.py:221
  58.3 28.0 %collective-permute-start.1 = (f32[320,128]{1,0:T(8,128)}, f32[320,128]{1,0:T(8,128)}, u32[]{:S(2)}, u32[]{:S(2)}) collective-permute-start(f32[320,128]{1,0:T(8,128)} %reshape.160), channel_id=1, source_target_pairs={{1,0},{2,1},{3,2},{4,3},{5,4},{6,5},{7,6},{8,7},{9,8},{10,9},{11,1... | collective-permute-start | bytes 491528 | tf_op jit(solution)/shard_map/ppermute | solution.py:222

commit v3 on v2

--- a/solution.py
+++ b/solution.py
@@ -118,7 +118,7 @@
     )
 
 
-def stencil_kernel(chunk, slab_rows, f_ref, r_ref, lo_ref, hi_ref, o_ref):
+def stencil_kernel(chunk, slab_rows, f_ref, r_ref, h_ref, o_ref):
     planes, piece = f_ref.shape[2], f_ref.shape[3]
     lane = lax.broadcasted_iota(jnp.int32, (planes, piece), 1)
     y_of = lane % chunk
@@ -130,22 +130,16 @@
 
     for k in range(f_ref.shape[1]):
 
-        def rim(c, side):
-            out = jnp.zeros((planes, piece), jnp.float32)
-            for row in range(slab_rows):
-                out = jnp.where(x_of == row, r_ref[c, k, side, row], out)
-            return out
-
         def moved(c, halo):
             f = f_ref[c, k]
-            y_up = jnp.where(last_y, rim(c, 1), pltpu.roll(f, piece - 1, 1))
-            y_down = jnp.where(first_y, rim(c, 0), pltpu.roll(f, 1, 1))
+            y_up = jnp.where(last_y, r_ref[c, k], pltpu.roll(f, piece - 1, 1))
+            y_down = jnp.where(first_y, r_ref[c, k], pltpu.roll(f, 1, 1))
             z_up = pltpu.roll(f, planes - 1, 0)
             z_down = pltpu.roll(f, 1, 0)
             if halo is None:
                 return f, y_up, y_down, z_up, z_down, None, None
-            x_up = jnp.where(last_x, hi_ref[halo, k], pltpu.roll(f, piece - chunk, 1))
-            x_down = jnp.where(first_x, lo_ref[halo, k], pltpu.roll(f, chunk, 1))
+            x_up = jnp.where(last_x, h_ref[halo, k], pltpu.roll(f, piece - chunk, 1))
+            x_down = jnp.where(first_x, h_ref[halo, k], pltpu.roll(f, chunk, 1))
             return f, y_up, y_down, z_up, z_down, x_up, x_down
 
         def laplace(c):
@@ -177,13 +171,16 @@
     both = jnp.stack([velocity, vorticity], axis=0).reshape(
         2, row_count, 3, slab_rows, group_count, chunk
     )
-    main = jnp.transpose(both, (4, 0, 2, 1, 3, 5)).reshape(group_count, -1)
-    left = jnp.roll(both[..., chunk - 1], 1, axis=4)
-    right = jnp.roll(both[..., 0], -1, axis=4)
-    rims = jnp.stack([left, right], axis=-1)
-    rims = jnp.transpose(rims, (4, 0, 2, 1, 3, 5)).reshape(group_count, -1)
-    main_len = main.shape[1]
-    sent = jnp.concatenate([main, rims], axis=1).reshape(group_count, -1, 128)
+    main = jnp.transpose(both, (4, 0, 2, 1, 3, 5)).reshape(group_count, -1, 128)
+    main_len = main.shape[1] * 128
+    column = np.arange(NY)
+    target = np.arange(group_count) * chunk
+    picks = np.stack([(target - 1) % NY, (target + chunk) % NY], axis=-1).reshape(-1)
+    select = jnp.asarray((column[:, None] == picks[None, :]).astype(np.float32))
+    rims = jnp.dot(both.reshape(-1, NY), select, precision=lax.Precision.HIGHEST)
+    rims = rims.reshape(2, row_count, 3, slab_rows, group_count, 2)
+    rims = jnp.transpose(rims, (4, 0, 2, 1, 3, 5)).reshape(group_count, -1, 128)
+    sent = jnp.concatenate([main, rims], axis=1)
     arrived = lax.all_to_all(sent, "mode", split_axis=0, concat_axis=0, tiled=True)
     arrived = arrived.reshape(group_count, -1)
     body = arrived[:, :main_len].reshape(MODES, halves, 2, 3, row_count, piece)
@@ -224,21 +221,28 @@
     high = high.reshape(x_shape)
 
     fields = jnp.stack(flux + damped, axis=0)
-    rims = jnp.stack(flux_rim + damped_rim, axis=0)
-    rims = jnp.transpose(rims, (0, 1, 4, 3, 2))[..., None]
-    low = jnp.tile(low, (1, 1, 1, slab_rows))
-    high = jnp.tile(high, (1, 1, 1, slab_rows))
+    rims = jnp.stack(flux_rim + damped_rim, axis=0).reshape(-1, slab_rows * 2)
+    lane = np.arange(piece)
+    slot = (lane // chunk) * 2 + (lane % chunk == chunk - 1)
+    edge_lane = (lane % chunk == 0) | (lane % chunk == chunk - 1)
+    place = (np.arange(slab_rows * 2)[:, None] == slot[None, :]) & edge_lane[None, :]
+    rims = jnp.dot(rims, jnp.asarray(place.astype(np.float32)), precision=lax.Precision.HIGHEST)
+    rims = rims.reshape(fields.shape)
+    width = piece - chunk
+    halo = jnp.pad(low, ((0, 0), (0, 0), (0, 0), (0, width))) + jnp.pad(
+        high, ((0, 0), (0, 0), (0, 0), (width, 0))
+    )
     rate = pl.pallas_call(
         functools.partial(stencil_kernel, chunk, slab_rows),
         out_shape=jax.ShapeDtypeStruct((MODES, 3, planes, piece), jnp.float32),
-        in_specs=[pl.BlockSpec(memory_space=pltpu.VMEM)] * 4,
+        in_specs=[pl.BlockSpec(memory_space=pltpu.VMEM)] * 3,
         out_specs=pl.BlockSpec(memory_space=pltpu.VMEM),
         cost_estimate=pl.CostEstimate(
             flops=MODES * 3 * planes * piece * 40,
-            bytes_accessed=(6 + 10 + 3) * MODES * planes * piece * 4,
+            bytes_accessed=(6 + 6 + 5 + 3) * MODES * planes * piece * 4,
             transcendentals=0,
         ),
-    )(fields, rims, low, high)
+    )(fields, rims, halo)
     rate = rate.reshape(MODES, 3, halves, row_count, piece)
     rate = jnp.transpose(rate, (0, 2, 1, 3, 4)).reshape(group_count, -1, 128)
     returned = lax.all_to_all(rate, "mode", split_axis=0, concat_axis=0, tiled=True)

time: 120 us -> 109 us (0.908)
  local copies, waits for them, and re-layouts: 33.1 us -> 18.1 us
  matrix products: 13.8 us -> 16.6 us
  other arithmetic: 1.54 us -> 3.69 us
  Pallas kernels: 4.48 us -> 2.9 us
    slice x6 -> x1, local copies, waits for them, and re-layouts: 6.32 us -> 0.15 us  [shards(): x_needs[..., piece - chunk:].reshape(-1, 128)]
    another operation x6 -> x0, local copies, waits for them, and re-layouts: 5.92 us -> none  [the longest x3 2.96 us: shards(): high = jnp.tile(high, (1, 1, 1, slab_rows))]
    broadcast_in_dim x1 -> x0, local copies, waits for them, and re-layouts: 3.56 us -> none  [shards(): rims = jnp.transpose(rims, (0, 1, 4, 3, 2))[..., None]]
    dot_general x0 -> x2, matrix products: none -> 2.55 us  [the longest x1 1.76 us: shards(): jnp.dot(rims, jnp.asarray(place.astype(np.float32)), precision=lax.Precis...]
    pallas_call x1, Pallas kernels: 4.48 us -> 2.9 us  [shards(): pl.pallas_call(functools.partial(stencil_kernel, chunk, slab_rows), out_s...]
    another operation x3 -> x4, local copies, waits for them, and re-layouts: 1.74 us -> 3.31 us  [shards(): jnp.stack([velocity, vorticity], axis=0)]
    reshape x3 -> x4, local copies, waits for them, and re-layouts: 3.13 us -> 2.91 us  [the longest x1 1.03 us: shards(): low = low.reshape(x_shape)]
  transfers between devices with their start and end apart: 3 -> 3, of which waited for: 1 -> 1; matrix products, arithmetic and copies ran while one was open for 17% -> 15% of each run, Pallas kernels for 0% -> 0%
where the time goes in v3:
time: 109 us; the launch traced here: 108 us
  starting transfers between devices  26.3 us (24%)
  waiting for transfers between devices  20 us (18%)
  blocking collectives  19.9 us (18%)
  local copies, waits for them, and re-layouts  18.1 us (17%)
  matrix products  16.6 us (15%)
  other arithmetic  3.69 us (3%)
  Pallas kernels  2.9 us (3%)
    all_to_all x1, waiting for transfers between devices, shards(): lax.all_to_all(sent, 'mode', split_axis=0, concat_axis=0, tiled=True)  20 us
    all_to_all x1, blocking collectives, shards(): lax.all_to_all(rate, 'mode', split_axis=0, concat_axis=0, tiled=True)  19.9 us
    all_to_all x1, starting transfers between devices, shards(): lax.all_to_all(sent, 'mode', split_axis=0, concat_axis=0, tiled=True)  12.8 us
    ppermute x1, starting transfers between devices, shards(): high = lax.ppermute(x_needs[..., :chunk].reshape(-1, 128), 'tile', backward)  11.3 us
    dot_general x6, matrix products, coupled(): jnp.dot(mixing_rows, spin[c].reshape(MODES, -1), precision=lax.Precision....  10.6 us
    dot_general x6, matrix products, coupled(): jnp.dot(flat_coupling, spin[c].reshape(MODES, -1), precision=lax.Precisio...  3.46 us
    another operation x4, local copies, waits for them, and re-layouts, shards(): jnp.stack([velocity, vorticity], axis=0)  3.31 us
    pallas_call x1, Pallas kernels, shards(): pl.pallas_call(functools.partial(stencil_kernel, chunk, slab_rows), out_s...  2.9 us
  transfers between devices with their start and end apart: 3, of which 1 were waited for; matrix products, arithmetic and copies ran while one was open for 15% of the time, Pallas kernels for 0%

profile of v3, /device:TPU:8, one launch (start us, length us, event | category | flops | bytes accessed | tf_op | source)
XLA Modules:
  0.0 107.9 jit_solution(3641933207075651692)
XLA Ops:
  0.0 1.4 %stack.44 = f32[1,8,3,4,16,64]{5,4,3,1,2,0:T(8,128)S(1)} reshape(f32[8,3,4096]{2,0,1:T(8,128)} %param.6) | data formatting | bytes 786432 | tf_op jit(solution)/shard_map/stack | solution.py:171
  1.4 1.3 %stack.45 = f32[1,8,3,4,16,64]{5,4,3,1,2,0:T(8,128)S(1)} reshape(f32[8,3,4096]{2,0,1:T(8,128)} %param.7) | data formatting | bytes 786432 | tf_op jit(solution)/shard_map/stack | solution.py:171
  2.7 0.8 convolution_bitcast_fusion
  3.5 0.1 copy.80
  3.7 0.1 copy.81
  3.8 0.3 copy.78
  4.1 0.3 copy.79
  4.4 0.4 maximum_bitcast_fusion
  4.8 0.8 reshape.183
  5.6 1.0 pad_maximum_fusion
  6.5 12.8 %all-to-all-start = ((f32[16,99,128]{2,1,0:T(8,128)}), f32[16,99,128]{2,1,0:T(8,128)S(1)}, u32[]{:S(2)}, u32[]{:S(2)}) async-start(f32[16,99,128]{2,1,0:T(8,128)} %pad_maximum_fusion), calls=%async_computation | async-start | bytes 1703936 | tf_op jit(solution)/shard_map/all_to_all | solution.py:184
  19.4 0.6 fusion.34
  20.0 20.0 %all-to-all-done = f32[16,99,128]{2,1,0:T(8,128)S(1)} async-done(((f32[16,99,128]{2,1,0:T(8,128)}), f32[16,99,128]{2,1,0:T(8,128)S(1)}, u32[]{:S(2)}, u32[]{:S(2)}) %all-to-all-start) | async-done | bytes 811040 | tf_op jit(solution)/shard_map/all_to_all | solution.py:184
  40.0 0.2 copy.177
  40.2 0.1 slice.124
  40.2 0.2 copy.140
  40.5 0.1 slice_bitcast_fusion.4
  40.6 0.1 copy.141
  40.7 0.3 copy-done.4
  40.9 1.6 %fusion.13 = f32[8,16,256]{2,0,1:T(8,128)S(1)} fusion(f32[1,8,8]{2,1,0:T(8,128)S(1)} %copy-done.4, f32[1,8,8]{2,1,0:T(8,128)S(1)} %copy-done.5, f32[]{:T(128)} %bitcast.20, f32[]{:T(128)} %bitcast.19, f32[1,8,16,256]{3,2,1,0:T(8,128)S(1)} %get-tuple-element.17), kind=kOutput, calls=%fused_computation.49 | convolution fusion | flops 3145920 | bytes 262664 | tf_op jit(solution)/shard_map/dot_general | solution.py:204
  42.6 1.6 %fusion.17 = f32[8,16,256]{2,0,1:T(8,128)S(1)} fusion(f32[1,8,8]{2,1,0:T(8,128)S(1)} %copy-done.4, f32[1,8,8]{2,1,0:T(8,128)S(1)} %copy-done.5, f32[]{:T(128)} %bitcast.20, f32[]{:T(128)} %bitcast.19, f32[1,8,16,256]{3,2,1,0:T(8,128)S(1)} %get-tuple-element.19), kind=kOutput, calls=%fused_computation.53 | convolution fusion | flops 3145920 | bytes 262664 | tf_op jit(solution)/shard_map/dot_general | solution.py:204
  44.2 0.1 copy.143
  44.3 1.6 %fusion.15 = f32[8,16,256]{2,0,1:T(8,128)S(1)} fusion(f32[1,8,8]{2,1,0:T(8,128)S(1)} %copy-done.4, f32[1,8,8]{2,1,0:T(8,128)S(1)} %copy-done.5, f32[]{:T(128)} %bitcast.20, f32[]{:T(128)} %bitcast.19, f32[1,8,16,256]{3,2,1,0:T(8,128)S(1)} %get-tuple-element.20), kind=kOutput, calls=%fused_computation.51 | convolution fusion | flops 3145920 | bytes 262664 | tf_op jit(solution)/shard_map/dot_general | solution.py:204
  45.9 0.1 copy.142
  46.0 0.9 fusion.42
  47.0 0.9 fusion.43
  47.9 0.9 fusion.41
  48.9 0.6 subtract_reduce_fusion
  49.8 0.2 fusion.33
  50.0 0.1 reshape.195
  50.1 0.8 reshape.197
  50.8 11.3 %collective-permute-start.1 = (f32[320,128]{1,0:T(8,128)}, f32[320,128]{1,0:T(8,128)}, u32[]{:S(2)}, u32[]{:S(2)}) collective-permute-start(f32[320,128]{1,0:T(8,128)} %reshape.197), channel_id=1, source_target_pairs={{1,0},{2,1},{3,2},{4,3},{5,4},{6,5},{7,6},{8,7},{9,8},{10,9},{11,1... | collective-permute-start | bytes 491528 | tf_op jit(solution)/shard_map/ppermute | solution.py:219
  62.2 2.1 %collective-permute-start = (f32[320,128]{1,0:T(8,128)S(1)}, f32[320,128]{1,0:T(8,128)}, u32[]{:S(2)}, u32[]{:S(2)}) collective-permute-start(f32[320,128]{1,0:T(8,128)S(1)} %reshape.195), channel_id=1, source_target_pairs={{0,1},{1,2},{2,3},{3,4},{4,5},{5,6},{6,7},{7,8},{8,9},{9,10},{10,1... | collective-permute-start | bytes 491528 | tf_op jit(solution)/shard_map/ppermute | solution.py:218
  64.3 2.0 %reshape.191 = f32[8,2,2,3,8,4,2]{6,5,4,3,2,1,0:T(4,128)S(1)} reshape(f32[16,384]{1,0:T(8,128)S(1)} %slice.131) | data formatting | bytes 49152 | tf_op jit(solution)/shard_map/reshape | solution.py:188
  66.3 0.2 fusion.32
  66.5 0.5 copy.92
  66.9 0.5 copy.100
  67.4 0.5 copy.98
  67.9 0.5 copy.95
  68.4 0.2 fusion.45
  68.6 0.2 fusion.46
  68.8 0.2 fusion.44
  69.0 0.5 copy.94
  69.5 0.5 copy.91
  70.0 0.2 reshape.192
  70.2 0.2 reshape.194
  70.4 0.2 reshape.193
  70.6 0.7 subtract_reduce_fusion.3
  71.3 0.1 copy.102
  71.4 0.1 copy.97
  71.5 0.1 copy.101
  71.6 1.9 %fusion.2 = f32[6,8,16,8]{2,1,3,0:T(8,128)S(1)} fusion(f32[6,8,16,8]{2,1,3,0:T(8,128)S(1)} %constant_dynamic-update-slice_fusion, f32[16,8,8]{2,1,0:T(8,128)S(1)} %bitcast.203, f32[1,8,8]{2,1,0:T(8,128)S(1)} %copy-done.4, f32[1,8,8]{2,1,0:T(8,128)S(1)} %copy-done.5, f32[]{:T(128)} %bitcast.20, f32[]{:T(128)} %bitcast.19), kind=kOutput, calls=%fused_computation.7 | convolution fusion | flops 98496 | bytes 106504 | tf_op jit(solution)/shard_map/dot_general | solution.py:204
  73.5 1.9 %fusion.1 = f32[6,8,16,8]{2,1,3,0:T(8,128)S(1)} fusion(f32[6,8,16,8]{2,1,3,0:T(8,128)S(1)} %fusion.2, f32[16,8,8]{2,1,0:T(8,128)S(1)} %bitcast.201, f32[1,8,8]{2,1,0:T(8,128)S(1)} %copy-done.4, f32[1,8,8]{2,1,0:T(8,128)S(1)} %copy-done.5, f32[]{:T(128)} %bitcast.20, f32[]{:T(128)} %bitcast.19), kind=kOutput, calls=%fused_computation.5 | convolution fusion | flops 98496 | bytes 106504 | tf_op jit(solution)/shard_map/dot_general | solution.py:204
  75.4 1.9 %fusion = f32[6,8,16,8]{2,1,3,0:T(8,128)S(1)} fusion(f32[6,8,16,8]{2,1,3,0:T(8,128)S(1)} %fusion.1, f32[16,8,8]{2,1,0:T(8,128)S(1)} %bitcast.199, f32[1,8,8]{2,1,0:T(8,128)S(1)} %copy-done.4, f32[1,8,8]{2,1,0:T(8,128)S(1)} %copy-done.5, f32[]{:T(128)} %bitcast.20, f32[]{:T(128)} %bitcast.19), kind=kOutput, calls=%fused_computation.3 | convolution fusion | flops 98496 | bytes 106504 | tf_op jit(solution)/shard_map/dot_general | solution.py:204
  77.4 1.8 %fusion.5.r_ref = f32[6,8,16,256]{3,2,1,0:T(8,128)} fusion(f32[8,256,1,1]{1,0,3,2:T(8,128)S(1)} %copy-done.7, f32[6,8,16,8]{2,1,3,0:T(8,128)S(1)} %fusion), kind=kOutput, calls=%fused_computation.21 | convolution fusion | flops 18874368 | bytes 819200 | tf_op jit(solution)/shard_map/dot_general | solution.py:229
  79.1 1.0 reshape.198
  80.2 1.0 reshape.196
  81.2 1.0 pad_add_fusion.h_ref
  82.2 2.9 %shard_map.64 = f32[8,3,16,256]{3,2,1,0:T(8,128)} custom-call(f32[6,8,16,256]{3,2,1,0:T(8,128)} %copy-done.3, f32[6,8,16,256]{3,2,1,0:T(8,128)} %fusion.5.r_ref, f32[5,8,16,256]{3,2,1,0:T(8,128)} %pad_add_fusion.h_ref), custom_call_target="tpu_custom_call" | custom-call | flops 3932160 | bytes 2621440 | tf_op jit(solution)/shard_map/pallas_call | solution.py:235
  85.1 1.0 copy_bitcast_fusion.1
  86.2 19.9 %all_to_all.10 = f32[16,48,128]{2,1,0:T(8,128)S(1)} all-to-all(f32[16,48,128]{2,1,0:T(8,128)S(1)} %reshape.200), channel_id=1, replica_groups=mesh['mode'=16,'tile'=48] {'mode'}, dimensions={0} | all-to-all | bytes 786432 | tf_op jit(solution)/shard_map/all_to_all | solution.py:248
  106.1 0.4 reshape.201
  106.4 0.5 copy.114
  106.9 1.0 reshape.202
  (30 shorter events, 0.4 us)
Async XLA Ops:
  0.0 2.7 %copy-start.6 = (f32[16,2,1024,1,1,1]{2,0,1,5,4,3:T(8,128)S(1)}, f32[16,2,1024,1,1,1]{2,0,1,5,4,3:T(8,128)}, u32[]{:S(2)}) copy-start(f32[16,2,1024,1,1,1]{2,0,1,5,4,3:T(8,128)} %constant.25) | copy-start | bytes 393220
  0.0 2.7 %copy-start.1 = (f32[8,3,4096]{2,0,1:T(8,128)S(1)}, f32[8,3,4096]{2,0,1:T(8,128)}, u32[]{:S(2)}) copy-start(f32[8,3,4096]{2,0,1:T(8,128)} %param.6) | copy-start | bytes 1179652
  0.0 2.7 %copy-start = (f32[8,3,4096]{2,0,1:T(8,128)S(1)}, f32[8,3,4096]{2,0,1:T(8,128)}, u32[]{:S(2)}) copy-start(f32[8,3,4096]{2,0,1:T(8,128)} %param.7) | copy-start | bytes 1179652
  5.6 13.8 %copy-start.8 = (f32[2]{0:T(128)S(1)}, f32[2]{0:T(128)}, u32[]{:S(2)}) copy-start(f32[2]{0:T(128)} %param.8) | copy-start | bytes 28
  6.5 33.5 %all-to-all-start = ((f32[16,99,128]{2,1,0:T(8,128)}), f32[16,99,128]{2,1,0:T(8,128)S(1)}, u32[]{:S(2)}, u32[]{:S(2)}) async-start(f32[16,99,128]{2,1,0:T(8,128)} %pad_maximum_fusion), calls=%async_computation | async-start | bytes 1703936 | tf_op jit(solution)/shard_map/all_to_all | solution.py:184
  40.2 0.7 copy-start.4
  40.2 0.7 copy-start.5
  40.5 5.5 %copy-start.2 = (f32[64,8]{1,0:T(8,128)S(1)}, f32[64,8]{1,0:T(8,128)}, u32[]{:S(2)}) copy-start(f32[64,8]{1,0:T(8,128)} %constant.22) | copy-start | bytes 6148
  49.8 16.5 %copy-start.3 = (f32[6,8,16,256]{3,2,1,0:T(8,128)}, f32[6,8,16,256]{3,2,1,0:T(8,128)S(1)}, u32[]{:S(2)}) copy-start(f32[6,8,16,256]{3,2,1,0:T(8,128)S(1)} %get-tuple-element.26.f_ref) | copy-start | bytes 2359300
  50.8 28.3 %collective-permute-start.1 = (f32[320,128]{1,0:T(8,128)}, f32[320,128]{1,0:T(8,128)}, u32[]{:S(2)}, u32[]{:S(2)}) collective-permute-start(f32[320,128]{1,0:T(8,128)} %reshape.197), channel_id=1, source_target_pairs={{1,0},{2,1},{3,2},{4,3},{5,4},{6,5},{7,6},{8,7},{9,8},{10,9},{11,1... | collective-permute-start | bytes 491528 | tf_op jit(solution)/shard_map/ppermute | solution.py:219
  62.2 18.0 %collective-permute-start = (f32[320,128]{1,0:T(8,128)S(1)}, f32[320,128]{1,0:T(8,128)}, u32[]{:S(2)}, u32[]{:S(2)}) collective-permute-start(f32[320,128]{1,0:T(8,128)S(1)} %reshape.195), channel_id=1, source_target_pairs={{0,1},{1,2},{2,3},{3,4},{4,5},{5,6},{6,7},{7,8},{8,9},{9,10},{10,1... | collective-permute-start | bytes 491528 | tf_op jit(solution)/shard_map/ppermute | solution.py:218
  70.4 7.0 %copy-start.7 = (f32[8,256,1,1]{1,0,3,2:T(8,128)S(1)}, f32[8,256,1,1]{1,0,3,2:T(8,128)}, u32[]{:S(2)}) copy-start(f32[8,256,1,1]{1,0,3,2:T(8,128)} %constant.26) | copy-start | bytes 24580

commit v4 on v3

--- a/solution.py
+++ b/solution.py
@@ -185,8 +185,8 @@
     arrived = arrived.reshape(group_count, -1)
     body = arrived[:, :main_len].reshape(MODES, halves, 2, 3, row_count, piece)
     body = jnp.transpose(body, (2, 3, 0, 1, 4, 5)).reshape(2, 3, MODES, planes, piece)
-    edge = arrived[:, main_len:].reshape(MODES, halves, 2, 3, row_count, slab_rows, 2)
-    edge = jnp.transpose(edge, (2, 3, 0, 1, 4, 5, 6)).reshape(2, 3, MODES, planes, slab_rows, 2)
+    edge = arrived[:, main_len:].reshape(MODES, halves, 2, 3, row_count * slab_rows * 2)
+    edge = jnp.transpose(edge, (2, 3, 0, 1, 4)).reshape(2, 3, MODES, planes * slab_rows * 2)
 
     def coupled(speed, spin):
         shape = spin.shape

time: 109 us -> 100 us (0.917)
  local copies, waits for them, and re-layouts: 18.1 us -> 11.5 us
  matrix products: 16.6 us -> 15.2 us
    reshape x4 -> x1, local copies, waits for them, and re-layouts: 2.54 us -> 0.09 us  [shards(): arrived[:, main_len:]]
    slice x5 -> x2, local copies, waits for them, and re-layouts: 1.6 us -> 0.17 us  [the longest x1 0.16 us: coupled(): speed[0][:, None] * mixed[2]]
    dot_general x6, matrix products: 10.6 us -> 9.34 us  [coupled(): jnp.dot(mixing_rows, spin[c].reshape(MODES, -1), precision=lax.Precision....]
  transfers between devices with their start and end apart: 3 -> 3, of which waited for: 1 -> 2; matrix products, arithmetic and copies ran while one was open for 15% -> 7% of each run, Pallas kernels for 0% -> 0%
where the time goes in v4:
time: 100 us; the launch traced here: 99.6 us
  starting transfers between devices  26.1 us (26%)
  waiting for transfers between devices  20.4 us (20%)
  blocking collectives  19.9 us (20%)
  matrix products  15.2 us (15%)
  local copies, waits for them, and re-layouts  11.5 us (12%)
  other arithmetic  3.13 us (3%)
  Pallas kernels  2.9 us (3%)
    all_to_all x1, waiting for transfers between devices, shards(): lax.all_to_all(sent, 'mode', split_axis=0, concat_axis=0, tiled=True)  20 us
    all_to_all x1, blocking collectives, shards(): lax.all_to_all(rate, 'mode', split_axis=0, concat_axis=0, tiled=True)  19.9 us
    all_to_all x1, starting transfers between devices, shards(): lax.all_to_all(sent, 'mode', split_axis=0, concat_axis=0, tiled=True)  12.8 us
    ppermute x1, starting transfers between devices, shards(): high = lax.ppermute(x_needs[..., :chunk].reshape(-1, 128), 'tile', backward)  11.3 us
    dot_general x6, matrix products, coupled(): jnp.dot(mixing_rows, spin[c].reshape(MODES, -1), precision=lax.Precision....  9.34 us
    dot_general x6, matrix products, coupled(): jnp.dot(flat_coupling, spin[c].reshape(MODES, -1), precision=lax.Precisio...  3.32 us
    another operation x4, local copies, waits for them, and re-layouts, shards(): jnp.stack([velocity, vorticity], axis=0)  3.31 us
    pallas_call x1, Pallas kernels, shards(): pl.pallas_call(functools.partial(stencil_kernel, chunk, slab_rows), out_s...  2.9 us
  transfers between devices with their start and end apart: 3, of which 2 were waited for; matrix products, arithmetic and copies ran while one was open for 7% of the time, Pallas kernels for 0%

profile of v4, /device:TPU:8, one launch (start us, length us, event | category | flops | bytes accessed | tf_op | source)
XLA Modules:
  0.0 99.6 jit_solution(17801874890874671380)
XLA Ops:
  0.0 1.4 %stack.47 = f32[1,8,3,4,16,64]{5,4,3,1,2,0:T(8,128)S(1)} reshape(f32[8,3,4096]{2,0,1:T(8,128)} %param.6) | data formatting | bytes 786432 | tf_op jit(solution)/shard_map/stack | solution.py:171
  1.4 1.3 %stack.48 = f32[1,8,3,4,16,64]{5,4,3,1,2,0:T(8,128)S(1)} reshape(f32[8,3,4096]{2,0,1:T(8,128)} %param.7) | data formatting | bytes 786432 | tf_op jit(solution)/shard_map/stack | solution.py:171
  2.7 0.8 convolution_bitcast_fusion
  3.5 0.1 copy.62
  3.7 0.1 copy.63
  3.8 0.3 copy.60
  4.1 0.3 copy.61
  4.4 0.4 maximum_bitcast_fusion
  4.8 0.8 reshape.165
  5.6 1.0 pad_maximum_fusion
  6.5 12.8 %all-to-all-start = ((f32[16,99,128]{2,1,0:T(8,128)}), f32[16,99,128]{2,1,0:T(8,128)S(1)}, u32[]{:S(2)}, u32[]{:S(2)}) async-start(f32[16,99,128]{2,1,0:T(8,128)} %pad_maximum_fusion), calls=%async_computation | async-start | bytes 1703936 | tf_op jit(solution)/shard_map/all_to_all | solution.py:184
  19.4 0.6 fusion.30
  20.0 20.0 %all-to-all-done = f32[16,99,128]{2,1,0:T(8,128)S(1)} async-done(((f32[16,99,128]{2,1,0:T(8,128)}), f32[16,99,128]{2,1,0:T(8,128)S(1)}, u32[]{:S(2)}, u32[]{:S(2)}) %all-to-all-start) | async-done | bytes 811040 | tf_op jit(solution)/shard_map/all_to_all | solution.py:184
  40.0 0.2 copy.132
  40.3 0.2 copy.101
  40.6 0.1 copy.102
  40.7 0.3 copy-done.4
  40.9 1.6 %fusion.10 = f32[8,16,256]{2,0,1:T(8,128)S(1)} fusion(f32[1,8,8]{2,1,0:T(8,128)S(1)} %copy-done.4, f32[1,8,8]{2,1,0:T(8,128)S(1)} %copy-done.5, f32[]{:T(128)} %bitcast.20, f32[]{:T(128)} %bitcast.19, f32[1,8,16,256]{3,2,1,0:T(8,128)S(1)} %get-tuple-element.17), kind=kOutput, calls=%fused_computation.55 | convolution fusion | flops 3145920 | bytes 262664 | tf_op jit(solution)/shard_map/dot_general | solution.py:204
  42.5 1.6 %fusion.14 = f32[8,16,256]{2,0,1:T(8,128)S(1)} fusion(f32[1,8,8]{2,1,0:T(8,128)S(1)} %copy-done.4, f32[1,8,8]{2,1,0:T(8,128)S(1)} %copy-done.5, f32[]{:T(128)} %bitcast.20, f32[]{:T(128)} %bitcast.19, f32[1,8,16,256]{3,2,1,0:T(8,128)S(1)} %get-tuple-element.19), kind=kOutput, calls=%fused_computation.59 | convolution fusion | flops 3145920 | bytes 262664 | tf_op jit(solution)/shard_map/dot_general | solution.py:204
  44.2 0.1 copy.104
  44.2 1.6 %fusion.12 = f32[8,16,256]{2,0,1:T(8,128)S(1)} fusion(f32[1,8,8]{2,1,0:T(8,128)S(1)} %copy-done.4, f32[1,8,8]{2,1,0:T(8,128)S(1)} %copy-done.5, f32[]{:T(128)} %bitcast.20, f32[]{:T(128)} %bitcast.19, f32[1,8,16,256]{3,2,1,0:T(8,128)S(1)} %get-tuple-element.20), kind=kOutput, calls=%fused_computation.57 | convolution fusion | flops 3145920 | bytes 262664 | tf_op jit(solution)/shard_map/dot_general | solution.py:204
  45.9 0.1 copy.103
  45.9 0.1 reshape.173
  46.0 0.2 slice_reduce_fusion
  46.2 0.1 mul.143
  46.3 0.1 squeeze.28
  46.7 0.2 convolution_bitcast_fusion.6
  46.8 0.2 convolution_bitcast_fusion.5
  47.0 0.2 subtract_reduce_fusion.3
  47.2 0.1 stack.59
  47.3 0.1 copy.81
  47.3 0.1 stack.57
  47.4 0.1 copy.79
  47.5 0.1 stack.58
  47.6 0.1 copy.80
  47.7 0.1 dot_general.130
  47.8 0.1 copy.78
  47.9 0.1 dot_general.126
  48.0 0.1 copy.76
  48.1 0.1 dot_general.122
  48.2 0.1 copy.74
  48.2 1.0 fusion.38
  49.2 0.9 fusion.39
  50.2 0.9 fusion.37
  51.1 0.7 subtract_reduce_fusion
  52.2 0.2 fusion.29
  52.4 0.1 reshape.177
  52.5 0.1 reshape.179
  52.6 11.3 %collective-permute-start.1 = (f32[320,128]{1,0:T(8,128)S(1)}, f32[320,128]{1,0:T(8,128)S(1)}, u32[]{:S(2)}, u32[]{:S(2)}) collective-permute-start(f32[320,128]{1,0:T(8,128)S(1)} %reshape.179), channel_id=1, source_target_pairs={{1,0},{2,1},{3,2},{4,3},{5,4},{6,5},{7,6},{8,7},{9,8},{10,9},{11,1... | collective-permute-start | bytes 491528 | tf_op jit(solution)/shard_map/ppermute | solution.py:219
  63.9 1.9 %collective-permute-start = (f32[320,128]{1,0:T(8,128)S(1)}, f32[320,128]{1,0:T(8,128)S(1)}, u32[]{:S(2)}, u32[]{:S(2)}) collective-permute-start(f32[320,128]{1,0:T(8,128)S(1)} %reshape.177), channel_id=1, source_target_pairs={{0,1},{1,2},{2,3},{3,4},{4,5},{5,6},{6,7},{7,8},{8,9},{9,10},{10,1... | collective-permute-start | bytes 491528 | tf_op jit(solution)/shard_map/ppermute | solution.py:218
  65.9 1.5 %fusion.2 = f32[6,8,16,8]{2,1,3,0:T(8,128)S(1)} fusion(f32[6,8,16,8]{2,1,3,0:T(8,128)S(1)} %constant_dynamic-update-slice_fusion, f32[16,8,8]{0,2,1:T(8,128)S(1)} %copy.74, f32[1,8,8]{2,1,0:T(8,128)S(1)} %copy-done.4, f32[1,8,8]{2,1,0:T(8,128)S(1)} %copy-done.5, f32[]{:T(128)} %bitcast.20, f32[]{:T(128)} %bitcast.19), kind=kOutput, calls=%fused_computation.7 | convolution fusion | flops 98496 | bytes 73736 | tf_op jit(solution)/shard_map/dot_general | solution.py:204
  67.4 1.5 %fusion.1 = f32[6,8,16,8]{2,1,3,0:T(8,128)S(1)} fusion(f32[6,8,16,8]{2,1,3,0:T(8,128)S(1)} %fusion.2, f32[16,8,8]{0,2,1:T(8,128)S(1)} %copy.76, f32[1,8,8]{2,1,0:T(8,128)S(1)} %copy-done.4, f32[1,8,8]{2,1,0:T(8,128)S(1)} %copy-done.5, f32[]{:T(128)} %bitcast.20, f32[]{:T(128)} %bitcast.19), kind=kOutput, calls=%fused_computation.5 | convolution fusion | flops 98496 | bytes 73736 | tf_op jit(solution)/shard_map/dot_general | solution.py:204
  68.9 1.5 %fusion = f32[6,8,16,8]{2,1,3,0:T(8,128)S(1)} fusion(f32[6,8,16,8]{2,1,3,0:T(8,128)S(1)} %fusion.1, f32[16,8,8]{0,2,1:T(8,128)S(1)} %copy.78, f32[1,8,8]{2,1,0:T(8,128)S(1)} %copy-done.4, f32[1,8,8]{2,1,0:T(8,128)S(1)} %copy-done.5, f32[]{:T(128)} %bitcast.20, f32[]{:T(128)} %bitcast.19), kind=kOutput, calls=%fused_computation.3 | convolution fusion | flops 98496 | bytes 73736 | tf_op jit(solution)/shard_map/dot_general | solution.py:204
  70.4 1.8 %fusion.5.r_ref = f32[6,8,16,256]{3,2,1,0:T(8,128)} fusion(f32[8,256,1,1]{1,0,3,2:T(8,128)S(1)} %copy-done.7, f32[6,8,16,8]{2,1,3,0:T(8,128)S(1)} %fusion), kind=kOutput, calls=%fused_computation.21 | convolution fusion | flops 18874368 | bytes 819200 | tf_op jit(solution)/shard_map/dot_general | solution.py:229
  72.2 0.1 reshape.180
  72.3 0.4 collective-permute-done
  72.7 0.1 reshape.178
  72.8 1.0 %pad_add_fusion.h_ref = f32[5,8,16,256]{3,2,1,0:T(8,128)} fusion(f32[5,8,16,64]{3,2,1,0:T(8,128)S(1)} %reshape.180, f32[5,8,16,64]{3,2,1,0:T(8,128)S(1)} %reshape.178), kind=kLoop, calls=%fused_computation.19 | loop fusion | flops 163840 | bytes 983040 | tf_op jit(solution)/shard_map/add | solution.py:232
  73.8 2.9 %shard_map.64 = f32[8,3,16,256]{3,2,1,0:T(8,128)} custom-call(f32[6,8,16,256]{3,2,1,0:T(8,128)} %copy-done.3, f32[6,8,16,256]{3,2,1,0:T(8,128)} %fusion.5.r_ref, f32[5,8,16,256]{3,2,1,0:T(8,128)} %pad_add_fusion.h_ref), custom_call_target="tpu_custom_call" | custom-call | flops 3932160 | bytes 2621440 | tf_op jit(solution)/shard_map/pallas_call | solution.py:235
  76.7 1.0 %copy_bitcast_fusion.1 = f32[8,2,3,8,256]{4,3,2,1,0:T(8,128)S(1)} fusion(f32[8,3,16,256]{3,2,1,0:T(8,128)} %shard_map.64), kind=kLoop, calls=%fused_computation.20 | loop fusion | bytes 786432 | tf_op jit(solution)/shard_map/transpose | solution.py:247
  77.8 19.9 %all_to_all.10 = f32[16,48,128]{2,1,0:T(8,128)S(1)} all-to-all(f32[16,48,128]{2,1,0:T(8,128)S(1)} %reshape.182), channel_id=1, replica_groups=mesh['mode'=16,'tile'=48] {'mode'}, dimensions={0} | all-to-all | bytes 786432 | tf_op jit(solution)/shard_map/all_to_all | solution.py:248
  97.7 0.4 reshape.183
  98.0 0.5 copy.84
  98.5 1.0 %reshape.184 = f32[8,3,4096]{2,0,1:T(8,128)} reshape(f32[8,3,4,16,64]{4,3,2,0,1:T(8,128)S(1)} %copy.84) | data formatting | bytes 786432 | tf_op jit(solution)/shard_map/reshape | solution.py:251
  (35 shorter events, 0.8 us)
Async XLA Ops:
  0.0 2.7 %copy-start.6 = (f32[16,2,1024,1,1,1]{2,0,1,5,4,3:T(8,128)S(1)}, f32[16,2,1024,1,1,1]{2,0,1,5,4,3:T(8,128)}, u32[]{:S(2)}) copy-start(f32[16,2,1024,1,1,1]{2,0,1,5,4,3:T(8,128)} %constant.25) | copy-start | bytes 393220
  0.0 2.7 %copy-start.1 = (f32[8,3,4096]{2,0,1:T(8,128)S(1)}, f32[8,3,4096]{2,0,1:T(8,128)}, u32[]{:S(2)}) copy-start(f32[8,3,4096]{2,0,1:T(8,128)} %param.6) | copy-start | bytes 1179652
  0.0 2.7 %copy-start = (f32[8,3,4096]{2,0,1:T(8,128)S(1)}, f32[8,3,4096]{2,0,1:T(8,128)}, u32[]{:S(2)}) copy-start(f32[8,3,4096]{2,0,1:T(8,128)} %param.7) | copy-start | bytes 1179652
  5.6 13.8 %copy-start.8 = (f32[2]{0:T(128)S(1)}, f32[2]{0:T(128)}, u32[]{:S(2)}) copy-start(f32[2]{0:T(128)} %param.8) | copy-start | bytes 28
  6.5 33.5 %all-to-all-start = ((f32[16,99,128]{2,1,0:T(8,128)}), f32[16,99,128]{2,1,0:T(8,128)S(1)}, u32[]{:S(2)}, u32[]{:S(2)}) async-start(f32[16,99,128]{2,1,0:T(8,128)} %pad_maximum_fusion), calls=%async_computation | async-start | bytes 1703936 | tf_op jit(solution)/shard_map/all_to_all | solution.py:184
  40.2 0.7 copy-start.4
  40.2 0.7 copy-start.5
  40.5 6.2 %copy-start.2 = (f32[64,8]{1,0:T(8,128)S(1)}, f32[64,8]{1,0:T(8,128)}, u32[]{:S(2)}) copy-start(f32[64,8]{1,0:T(8,128)} %constant.22) | copy-start | bytes 6148
  52.1 18.3 %copy-start.7 = (f32[8,256,1,1]{1,0,3,2:T(8,128)S(1)}, f32[8,256,1,1]{1,0,3,2:T(8,128)}, u32[]{:S(2)}) copy-start(f32[8,256,1,1]{1,0,3,2:T(8,128)} %constant.26) | copy-start | bytes 24580
  52.2 20.0 %copy-start.3 = (f32[6,8,16,256]{3,2,1,0:T(8,128)}, f32[6,8,16,256]{3,2,1,0:T(8,128)S(1)}, u32[]{:S(2)}) copy-start(f32[6,8,16,256]{3,2,1,0:T(8,128)S(1)} %get-tuple-element.26.f_ref) | copy-start | bytes 2359300
  52.6 19.6 %collective-permute-start.1 = (f32[320,128]{1,0:T(8,128)S(1)}, f32[320,128]{1,0:T(8,128)S(1)}, u32[]{:S(2)}, u32[]{:S(2)}) collective-permute-start(f32[320,128]{1,0:T(8,128)S(1)} %reshape.179), channel_id=1, source_target_pairs={{1,0},{2,1},{3,2},{4,3},{5,4},{6,5},{7,6},{8,7},{9,8},{10,9},{11,1... | collective-permute-start | bytes 491528 | tf_op jit(solution)/shard_map/ppermute | solution.py:219
  63.9 8.7 %collective-permute-start = (f32[320,128]{1,0:T(8,128)S(1)}, f32[320,128]{1,0:T(8,128)S(1)}, u32[]{:S(2)}, u32[]{:S(2)}) collective-permute-start(f32[320,128]{1,0:T(8,128)S(1)} %reshape.177), channel_id=1, source_target_pairs={{0,1},{1,2},{2,3},{3,4},{4,5},{5,6},{6,7},{7,8},{8,9},{9,10},{10,1... | collective-permute-start | bytes 491528 | tf_op jit(solution)/shard_map/ppermute | solution.py:218

commit v5 on v4

--- a/solution.py
+++ b/solution.py
@@ -221,13 +221,15 @@
     high = high.reshape(x_shape)
 
     fields = jnp.stack(flux + damped, axis=0)
-    rims = jnp.stack(flux_rim + damped_rim, axis=0).reshape(-1, slab_rows * 2)
-    lane = np.arange(piece)
-    slot = (lane // chunk) * 2 + (lane % chunk == chunk - 1)
+    rims = lax.optimization_barrier(jnp.stack(flux_rim + damped_rim, axis=0))
+    rims = rims.reshape(6, MODES, planes, slab_rows * 2)
+    lane = lax.broadcasted_iota(jnp.int32, (1, 1, 1, piece), 3)
+    slot = (lane // chunk) * 2 + (lane % chunk == chunk - 1).astype(jnp.int32)
     edge_lane = (lane % chunk == 0) | (lane % chunk == chunk - 1)
-    place = (np.arange(slab_rows * 2)[:, None] == slot[None, :]) & edge_lane[None, :]
-    rims = jnp.dot(rims, jnp.asarray(place.astype(np.float32)), precision=lax.Precision.HIGHEST)
-    rims = rims.reshape(fields.shape)
+    placed = jnp.zeros(fields.shape, jnp.float32)
+    for number in range(slab_rows * 2):
+        placed = jnp.where(edge_lane & (slot == number), rims[..., number : number + 1], placed)
+    rims = placed
     width = piece - chunk
     halo = jnp.pad(low, ((0, 0), (0, 0), (0, 0), (0, width))) + jnp.pad(
         high, ((0, 0), (0, 0), (0, 0), (width, 0))

time: 100 us -> 105 us (1.050)
  waiting for transfers between devices: 20.4 us -> 24.7 us
  matrix products: 15.2 us -> 13.3 us
  other arithmetic: 3.13 us -> 4.91 us
    ppermute x1, waiting for transfers between devices: 0.35 us -> 4.76 us  [shards(): lax.ppermute(x_needs[..., piece - chunk:].reshape(-1, 128), 'tile', forward)]
    dot_general x1 -> x0, matrix products: 1.77 us -> none  [shards(): jnp.dot(rims, jnp.asarray(place.astype(np.float32)), precision=lax.Precis...]
    select_n x0 -> x1, other arithmetic: none -> 1.75 us  [shards(): jnp.where(edge_lane & (slot == number), rims[..., number:number + 1], pla...]
    slice x0 -> x1, local copies, waits for them, and re-layouts: none -> 1.61 us  [shards(): rims[..., number:number + 1]]
  transfers between devices with their start and end apart: 3 -> 3, of which waited for: 2 -> 2; matrix products, arithmetic and copies ran while one was open for 7% -> 2% of each run, Pallas kernels for 0% -> 0%
where the time goes in v5:
time: 105 us
  starting transfers between devices  26.3 us (25%)
  waiting for transfers between devices  24.7 us (24%)
  blocking collectives  19.9 us (19%)
  matrix products  13.3 us (13%)
  local copies, waits for them, and re-layouts  12.3 us (12%)
  other arithmetic  4.91 us (5%)
  Pallas kernels  2.9 us (3%)
    all_to_all x1, waiting for transfers between devices, shards(): lax.all_to_all(sent, 'mode', split_axis=0, concat_axis=0, tiled=True)  19.9 us
    all_to_all x1, blocking collectives, shards(): lax.all_to_all(rate, 'mode', split_axis=0, concat_axis=0, tiled=True)  19.9 us
    all_to_all x1, starting transfers between devices, shards(): lax.all_to_all(sent, 'mode', split_axis=0, concat_axis=0, tiled=True)  12.8 us
    ppermute x1, starting transfers between devices, shards(): high = lax.ppermute(x_needs[..., :chunk].reshape(-1, 128), 'tile', backward)  11.3 us
    dot_general x6, matrix products, coupled(): jnp.dot(mixing_rows, spin[c].reshape(MODES, -1), precision=lax.Precision....  9.24 us
    ppermute x1, waiting for transfers between devices, shards(): lax.ppermute(x_needs[..., piece - chunk:].reshape(-1, 128), 'tile', forward)  4.76 us
    dot_general x6, matrix products, coupled(): jnp.dot(flat_coupling, spin[c].reshape(MODES, -1), precision=lax.Precisio...  3.31 us
    another operation x4, local copies, waits for them, and re-layouts, shards(): jnp.stack([velocity, vorticity], axis=0)  3.31 us
  transfers between devices with their start and end apart: 3, of which 2 were waited for; matrix products, arithmetic and copies ran while one was open for 2% of the time, Pallas kernels for 0%

profile of v5, /device:TPU:8, one launch (start us, length us, event | category | flops | bytes accessed | tf_op | source)
XLA Modules:
  0.0 104.8 jit_solution(8829333805764699493)
XLA Ops:
  0.0 1.4 %stack.53 = f32[1,8,3,4,16,64]{5,4,3,1,2,0:T(8,128)S(1)} reshape(f32[8,3,4096]{2,0,1:T(8,128)} %param.5) | data formatting | bytes 786432 | tf_op jit(solution)/shard_map/stack | solution.py:171
  1.4 1.3 %stack.54 = f32[1,8,3,4,16,64]{5,4,3,1,2,0:T(8,128)S(1)} reshape(f32[8,3,4096]{2,0,1:T(8,128)} %param.6) | data formatting | bytes 786432 | tf_op jit(solution)/shard_map/stack | solution.py:171
  2.7 0.8 convolution_bitcast_fusion
  3.5 0.1 copy.45
  3.7 0.1 copy.46
  3.8 0.3 copy.43
  4.1 0.3 copy.44
  4.4 0.4 maximum_bitcast_fusion
  4.8 0.8 reshape.239
  5.6 1.0 pad_maximum_fusion
  6.5 12.8 %all-to-all-start = ((f32[16,99,128]{2,1,0:T(8,128)}), f32[16,99,128]{2,1,0:T(8,128)S(1)}, u32[]{:S(2)}, u32[]{:S(2)}) async-start(f32[16,99,128]{2,1,0:T(8,128)} %pad_maximum_fusion), calls=%async_computation | async-start | bytes 1703936 | tf_op jit(solution)/shard_map/all_to_all | solution.py:184
  19.4 0.6 fusion.32
  20.1 19.9 %all-to-all-done = f32[16,99,128]{2,1,0:T(8,128)S(1)} async-done(((f32[16,99,128]{2,1,0:T(8,128)}), f32[16,99,128]{2,1,0:T(8,128)S(1)}, u32[]{:S(2)}, u32[]{:S(2)}) %all-to-all-start) | async-done | bytes 811040 | tf_op jit(solution)/shard_map/all_to_all | solution.py:184
  40.0 0.2 copy.96
  40.2 0.1 slice.156
  40.2 0.0 copy-start.4
  40.2 0.0 copy-start.5
  40.3 0.2 copy.67
  40.5 0.0 copy-start.2
  40.5 0.1 slice_bitcast_fusion.4
  40.6 0.1 copy.68
  40.7 0.3 copy-done.4
  40.9 0.0 copy-done.5
  40.9 1.6 %fusion.5 = f32[8,16,256]{2,0,1:T(8,128)S(1)} fusion(f32[1,8,8]{2,1,0:T(8,128)S(1)} %copy-done.4, f32[1,8,8]{2,1,0:T(8,128)S(1)} %copy-done.5, f32[]{:T(128)} %bitcast.20, f32[]{:T(128)} %bitcast.19, f32[1,8,16,256]{3,2,1,0:T(8,128)S(1)} %get-tuple-element.25), kind=kOutput, calls=%fused_computation.59 | convolution fusion | flops 3145920 | bytes 262664 | tf_op jit(solution)/shard_map/dot_general | solution.py:204
  42.5 1.6 %fusion.9 = f32[8,16,256]{2,0,1:T(8,128)S(1)} fusion(f32[1,8,8]{2,1,0:T(8,128)S(1)} %copy-done.4, f32[1,8,8]{2,1,0:T(8,128)S(1)} %copy-done.5, f32[]{:T(128)} %bitcast.20, f32[]{:T(128)} %bitcast.19, f32[1,8,16,256]{3,2,1,0:T(8,128)S(1)} %get-tuple-element.27), kind=kOutput, calls=%fused_computation.63 | convolution fusion | flops 3145920 | bytes 262664 | tf_op jit(solution)/shard_map/dot_general | solution.py:204
  44.2 0.1 copy.70
  44.2 1.6 %fusion.7 = f32[8,16,256]{2,0,1:T(8,128)S(1)} fusion(f32[1,8,8]{2,1,0:T(8,128)S(1)} %copy-done.4, f32[1,8,8]{2,1,0:T(8,128)S(1)} %copy-done.5, f32[]{:T(128)} %bitcast.20, f32[]{:T(128)} %bitcast.19, f32[1,8,16,256]{3,2,1,0:T(8,128)S(1)} %get-tuple-element.28), kind=kOutput, calls=%fused_computation.61 | convolution fusion | flops 3145920 | bytes 262664 | tf_op jit(solution)/shard_map/dot_general | solution.py:204
  45.9 0.1 copy.69
  45.9 0.1 reshape.247
  46.0 0.2 slice_reduce_fusion.8
  46.2 0.1 mul.187
  46.3 0.1 squeeze.28
  46.4 0.1 squeeze.13
  46.4 0.1 squeeze.12
  46.5 0.1 mul.183
  46.6 0.1 mul.180
  46.7 0.2 convolution_bitcast_fusion.3
  46.8 0.2 convolution_bitcast_fusion.2
  47.0 0.2 subtract_reduce_fusion.3
  47.2 1.5 %fusion.2 = f32[6,8,128]{2,1,0:T(8,128)S(1)} fusion(f32[6,8,128]{2,1,0:T(8,128)S(1)} %constant_dynamic-update-slice_fusion, f32[8,128]{1,0:T(8,128)S(1)} %squeeze.28, f32[1,8,8]{2,1,0:T(8,128)S(1)} %copy-done.4, f32[1,8,8]{2,1,0:T(8,128)S(1)} %copy-done.5, f32[]{:T(128)} %bitcast.20, f32[]{:T(128)} %bitcast.19), kind=kOutput, calls=%fused_computation.10 | convolution fusion | flops 98496 | bytes 16392 | tf_op jit(solution)/shard_map/dot_general | solution.py:204
  48.7 1.5 %fusion.1 = f32[6,8,128]{2,1,0:T(8,128)S(1)} fusion(f32[6,8,128]{2,1,0:T(8,128)S(1)} %fusion.2, f32[8,128]{1,0:T(8,128)S(1)} %squeeze.13, f32[1,8,8]{2,1,0:T(8,128)S(1)} %copy-done.4, f32[1,8,8]{2,1,0:T(8,128)S(1)} %copy-done.5, f32[]{:T(128)} %bitcast.20, f32[]{:T(128)} %bitcast.19), kind=kOutput, calls=%fused_computation.8 | convolution fusion | flops 98496 | bytes 16392 | tf_op jit(solution)/shard_map/dot_general | solution.py:204
  50.2 1.5 %fusion = f32[6,8,128]{2,1,0:T(8,128)S(1)} fusion(f32[6,8,128]{2,1,0:T(8,128)S(1)} %fusion.1, f32[8,128]{1,0:T(8,128)S(1)} %squeeze.12, f32[1,8,8]{2,1,0:T(8,128)S(1)} %copy-done.4, f32[1,8,8]{2,1,0:T(8,128)S(1)} %copy-done.5, f32[]{:T(128)} %bitcast.20, f32[]{:T(128)} %bitcast.19), kind=kOutput, calls=%fused_computation.6 | convolution fusion | flops 98496 | bytes 16392 | tf_op jit(solution)/shard_map/dot_general | solution.py:204
  51.6 0.2 reshape.251
  51.9 1.6 %slice_reduce_fusion.7 = (f32[6,8,16]{2,1,0:T(8,128)S(1)}, f32[6,8,16]{2,1,0:T(8,128)S(1)}, f32[6,8,16]{2,1,0:T(8,128)S(1)}, f32[6,8,16]{2,1,0:T(8,128)S(1)}, f3...) fusion(f32[6,8,16,8]{3,2,1,0:T(8,128)S(1)} %reshape.251), kind=kLoop, calls=%fused_computation.28 | loop fusion | bytes 49152 | tf_op jit(solution)/shard_map/slice | solution.py:231
  53.5 0.9 fusion.40
  54.5 0.9 fusion.41
  55.4 0.9 fusion.39
  56.4 0.7 subtract_reduce_fusion
  57.4 0.2 fusion.31
  57.6 0.1 reshape.252
  57.7 0.1 reshape.254
  57.8 11.3 %collective-permute-start.1 = (f32[320,128]{1,0:T(8,128)S(1)}, f32[320,128]{1,0:T(8,128)S(1)}, u32[]{:S(2)}, u32[]{:S(2)}) collective-permute-start(f32[320,128]{1,0:T(8,128)S(1)} %reshape.254), channel_id=1, source_target_pairs={{1,0},{2,1},{3,2},{4,3},{5,4},{6,5},{7,6},{8,7},{9,8},{10,9},{11,1... | collective-permute-start | bytes 491528 | tf_op jit(solution)/shard_map/ppermute | solution.py:219
  69.2 2.1 %collective-permute-start = (f32[320,128]{1,0:T(8,128)S(1)}, f32[320,128]{1,0:T(8,128)S(1)}, u32[]{:S(2)}, u32[]{:S(2)}) collective-permute-start(f32[320,128]{1,0:T(8,128)S(1)} %reshape.252), channel_id=1, source_target_pairs={{0,1},{1,2},{2,3},{3,4},{4,5},{5,6},{6,7},{7,8},{8,9},{9,10},{10,1... | collective-permute-start | bytes 491528 | tf_op jit(solution)/shard_map/ppermute | solution.py:218
  71.3 1.7 %select_select_fusion.r_ref = f32[6,8,16,256]{3,2,1,0:T(8,128)} fusion(f32[6,8,16]{2,1,0:T(8,128)S(1)} %get-tuple-element.9, f32[6,8,16]{2,1,0:T(8,128)S(1)} %get-tuple-element.10, f32[6,8,16]{2,1,0:T(8,128)S(1)} %get-tuple-element.11, f32[6,8,16]{2,1,0:T(8,128)S(1)} %get-tuple-element.12, f32[6,8,16]{2,1,0:T(8,128)S(1)} %get-tuple-element.13, ...), kind=kLoop, calls=%fused_computation.19 | loop fusion | flops 1572864 | bytes 813056 | tf_op jit(solution)/shard_map/jit(_where)/select_n | solution.py:231
  73.0 0.1 reshape.255
  73.1 4.8 %collective-permute-done = f32[320,128]{1,0:T(8,128)S(1)} collective-permute-done((f32[320,128]{1,0:T(8,128)S(1)}, f32[320,128]{1,0:T(8,128)S(1)}, u32[]{:S(2)}, u32[]{:S(2)}) %collective-permute-start) | collective-permute-done | bytes 163872 | tf_op jit(solution)/shard_map/ppermute | solution.py:218
  77.9 0.1 reshape.253
  78.0 1.0 pad_add_fusion.h_ref
  79.0 2.9 %shard_map.55 = f32[8,3,16,256]{3,2,1,0:T(8,128)} custom-call(f32[6,8,16,256]{3,2,1,0:T(8,128)} %copy-done.3, f32[6,8,16,256]{3,2,1,0:T(8,128)} %select_select_fusion.r_ref, f32[5,8,16,256]{3,2,1,0:T(8,128)} %pad_add_fusion.h_ref), custom_call_target="tpu_custom_call" | custom-call | flops 3932160 | bytes 2621440 | tf_op jit(solution)/shard_map/pallas_call | solution.py:237
  81.9 1.0 copy_bitcast_fusion.1
  83.0 19.9 %all_to_all.10 = f32[16,48,128]{2,1,0:T(8,128)S(1)} all-to-all(f32[16,48,128]{2,1,0:T(8,128)S(1)} %reshape.257), channel_id=1, replica_groups=mesh['mode'=16,'tile'=48] {'mode'}, dimensions={0} | all-to-all | bytes 786432 | tf_op jit(solution)/shard_map/all_to_all | solution.py:250
  102.9 0.4 reshape.258
  103.3 0.5 copy.57
  103.8 1.0 reshape.259
  (27 shorter events, 0.4 us)
Async XLA Ops:
  0.0 2.7 %copy-start.6 = (f32[16,2,1024,1,1,1]{2,0,1,5,4,3:T(8,128)S(1)}, f32[16,2,1024,1,1,1]{2,0,1,5,4,3:T(8,128)}, u32[]{:S(2)}) copy-start(f32[16,2,1024,1,1,1]{2,0,1,5,4,3:T(8,128)} %constant.88) | copy-start | bytes 393220
  0.0 2.7 %copy-start.1 = (f32[8,3,4096]{2,0,1:T(8,128)S(1)}, f32[8,3,4096]{2,0,1:T(8,128)}, u32[]{:S(2)}) copy-start(f32[8,3,4096]{2,0,1:T(8,128)} %param.5) | copy-start | bytes 1179652
  0.0 2.7 %copy-start = (f32[8,3,4096]{2,0,1:T(8,128)S(1)}, f32[8,3,4096]{2,0,1:T(8,128)}, u32[]{:S(2)}) copy-start(f32[8,3,4096]{2,0,1:T(8,128)} %param.6) | copy-start | bytes 1179652
  5.6 13.9 %copy-start.7 = (f32[2]{0:T(128)S(1)}, f32[2]{0:T(128)}, u32[]{:S(2)}) copy-start(f32[2]{0:T(128)} %param.7) | copy-start | bytes 28
  6.5 33.5 %all-to-all-start = ((f32[16,99,128]{2,1,0:T(8,128)}), f32[16,99,128]{2,1,0:T(8,128)S(1)}, u32[]{:S(2)}, u32[]{:S(2)}) async-start(f32[16,99,128]{2,1,0:T(8,128)} %pad_maximum_fusion), calls=%async_computation | async-start | bytes 1703936 | tf_op jit(solution)/shard_map/all_to_all | solution.py:184
  40.2 0.7 copy-start.4
  40.2 0.7 copy-start.5
  40.5 6.2 %copy-start.2 = (f32[64,8]{1,0:T(8,128)S(1)}, f32[64,8]{1,0:T(8,128)}, u32[]{:S(2)}) copy-start(f32[64,8]{1,0:T(8,128)} %constant.85) | copy-start | bytes 6148
  57.4 15.6 %copy-start.3 = (f32[6,8,16,256]{3,2,1,0:T(8,128)}, f32[6,8,16,256]{3,2,1,0:T(8,128)S(1)}, u32[]{:S(2)}) copy-start(f32[6,8,16,256]{3,2,1,0:T(8,128)S(1)} %get-tuple-element.34.f_ref) | copy-start | bytes 2359300
  57.8 15.2 %collective-permute-start.1 = (f32[320,128]{1,0:T(8,128)S(1)}, f32[320,128]{1,0:T(8,128)S(1)}, u32[]{:S(2)}, u32[]{:S(2)}) collective-permute-start(f32[320,128]{1,0:T(8,128)S(1)} %reshape.254), channel_id=1, source_target_pairs={{1,0},{2,1},{3,2},{4,3},{5,4},{6,5},{7,6},{8,7},{9,8},{10,9},{11,1... | collective-permute-start | bytes 491528 | tf_op jit(solution)/shard_map/ppermute | solution.py:219
  69.2 8.7 %collective-permute-start = (f32[320,128]{1,0:T(8,128)S(1)}, f32[320,128]{1,0:T(8,128)S(1)}, u32[]{:S(2)}, u32[]{:S(2)}) collective-permute-start(f32[320,128]{1,0:T(8,128)S(1)} %reshape.252), channel_id=1, source_target_pairs={{0,1},{1,2},{2,3},{3,4},{4,5},{5,6},{6,7},{7,8},{8,9},{9,10},{10,1... | collective-permute-start | bytes 491528 | tf_op jit(solution)/shard_map/ppermute | solution.py:218
